TPU v7x, 128 devices: a whole 4x4x4 slice. The times are simulated.
128 devices in a mesh: section: 4 (over x), tensor: 16 (over y, z), dp: 2 (over core).
Axes of the slice: x: 4, y: 4, z: 4, core: 2. Of those that a mesh axis runs over, the one named last changes fastest.
Arguments:
- patches: bfloat16 [1536, 8192], P(('section', 'dp'), 'tensor'), may hold values from -12 to 12
- teacher: bfloat16 [1536, 8192], P(('section', 'dp'), 'tensor'), may hold values from -6 to 6
- critic_pairs: int32 [1536, 2], P(('section', 'dp')), may hold values from 0 to 3, as said below
- left_factors: bfloat16 [4, 4, 64, 128, 128], P('section', None, 'tensor'), may hold values from -0.5 to 0.5
- right_factors: bfloat16 [4, 4, 64, 128, 128], P('section', None, 'tensor'), may hold values from -0.5 to 0.5
- norm_gains: bfloat16 [4, 5, 8192], P('section', None, 'tensor'), may hold values from 0.099609375 to 1.8984375
Outputs:
- d_patches: bfloat16 [1536, 8192], P(('section', 'dp'), 'tensor')
- grad_left: float32 [4, 4, 64, 128, 128], P('section', None, 'tensor')
- grad_right: float32 [4, 4, 64, 128, 128], P('section', None, 'tensor')
Inputs may be any that keep to these rules, and one draw needn't show every extreme that they name: `critic_pairs`: each row names two different critics. The rows are cut into aligned blocks, each block being the 192 rows of one index of section+dp. In each block, exactly one third of the rows name the pair of critics 0 and 1. Exactly one sixth of the rows name each of the pairs 0 and 2, 0 and 3, 1 and 2, and 1 and 3. No row names critics 2 and 3 together. So critics 0 and 1 are each named by two thirds of a block's rows, and critics 2 and 3 by one third each. Which rows and which column order are random.
All inputs are finite; a program needn't handle non-finite values.
Results may differ from a plain program's by a relative error of at most 0.012.
Values may be sent and summed in bfloat16 or wider, within the bound.
A program may use at most 64 MiB of HBM per device.

v0:
```python
import math

import jax
import jax.numpy as jnp
from jax import lax
from jax.sharding import PartitionSpec as P

EPSILON = 1e-06
TANH_SLOPE = 0.7978845608028654
CUBIC_TERM = 0.044715


def gelu_value(values):
    tangent = jnp.tanh(TANH_SLOPE * (values + CUBIC_TERM * values * values * values))
    return 0.5 * values * (1.0 + tangent)


def gelu_slope(values):
    tangent = jnp.tanh(TANH_SLOPE * (values + CUBIC_TERM * values * values * values))
    return 0.5 * (1.0 + tangent) + 0.5 * values * (1.0 - tangent * tangent) * TANH_SLOPE * (
        1.0 + 3.0 * CUBIC_TERM * values * values
    )


def norm_pair(residuals, gain_pair, model_width):
    squares = lax.psum(
        (
            jnp.sum(residuals[0] * residuals[0], axis=(1, 2)),
            jnp.sum(residuals[1] * residuals[1], axis=(1, 2)),
        ),
        "tensor",
    )
    factors = [lax.rsqrt(squares[member] / model_width + EPSILON) for member in range(2)]
    normed = [
        residuals[member] * factors[member][:, None, None] * gain_pair[member][None]
        for member in range(2)
    ]
    return (factors, normed)


def norm_back_pair(residuals, factors, gain_pair, grad_normed, carried, model_width):
    weighted = [grad_normed[member] * gain_pair[member][None] for member in range(2)]
    inners = lax.psum(
        (
            jnp.sum(weighted[0] * residuals[0], axis=(1, 2)),
            jnp.sum(weighted[1] * residuals[1], axis=(1, 2)),
        ),
        "tensor",
    )
    return [
        carried[member]
        + factors[member][:, None, None] * weighted[member]
        - residuals[member] * (factors[member] ** 3 * inners[member] / model_width)[:, None, None]
        for member in range(2)
    ]


def shards(patches, teacher, critic_pairs, left_factors, right_factors, norm_gains):
    sections = lax.axis_size("section")
    tensor_width = lax.axis_size("tensor")
    replicas = lax.axis_size("dp")
    tok_rows = patches.shape[0]
    feat_local = patches.shape[1]
    layer_count = left_factors.shape[1]
    local_blocks = left_factors.shape[2]
    block_size = left_factors.shape[3]
    all_blocks = local_blocks * tensor_width
    fold_ratio = block_size // all_blocks
    model_width = feat_local * tensor_width
    sixth_rows = tok_rows // 6
    leading = 2 * sixth_rows
    critic_ids = jnp.arange(4, dtype=jnp.int32)
    named_by = (
        (critic_pairs[:, 0:1] == critic_ids[None, :])
        | (critic_pairs[:, 1:2] == critic_ids[None, :])
    ).astype(jnp.int32)
    ranking = jnp.cumsum(named_by, axis=0) - 1
    slot_width = 4 * sixth_rows
    destination = jnp.broadcast_to(critic_ids[None, :], ranking.shape)
    flat_slot = destination * slot_width + ranking
    chosen = jnp.take_along_axis(flat_slot, critic_pairs, axis=1)
    slot_total = sections * slot_width
    row_ids = jnp.broadcast_to(jnp.arange(tok_rows, dtype=jnp.int32)[:, None], chosen.shape)
    source_row = (
        jnp.full((slot_total,), tok_rows, jnp.int32).at[chosen.reshape(-1)].set(row_ids.reshape(-1))
    )
    send_patch = (
        patches.at[source_row]
        .get(mode="fill", fill_value=0)
        .reshape(sections, slot_width, local_blocks, block_size)
    )
    send_target = (
        teacher.at[source_row]
        .get(mode="fill", fill_value=0)
        .reshape(sections, slot_width, local_blocks, block_size)
    )
    recv_patch, recv_target = (
        lax.all_to_all(send_patch, "section", split_axis=0, concat_axis=0, tiled=True),
        lax.all_to_all(send_target, "section", split_axis=0, concat_axis=0, tiled=True),
    )
    residuals = [
        recv_patch[:, :leading].reshape(-1, local_blocks, block_size).astype(jnp.float32),
        recv_patch[:, leading:].reshape(-1, local_blocks, block_size).astype(jnp.float32),
    ]
    targets = [
        recv_target[:, :leading].reshape(-1, local_blocks, block_size).astype(jnp.float32),
        recv_target[:, leading:].reshape(-1, local_blocks, block_size).astype(jnp.float32),
    ]
    native = (left_factors[0], right_factors[0], norm_gains[0])
    left_sets = (native[0], native[0])
    right_sets = (native[1], native[1])
    gain_sets = (
        native[2].astype(jnp.float32).reshape(layer_count + 1, local_blocks, block_size),
        native[2].astype(jnp.float32).reshape(layer_count + 1, local_blocks, block_size),
    )
    stored = []
    for layer_index in range(layer_count):
        gain_pair = [gain_sets[0][layer_index], gain_sets[1][layer_index]]
        factors, normed = norm_pair(residuals, gain_pair, model_width)
        normed = [normed[member].astype(jnp.bfloat16) for member in range(2)]
        first_out = [
            jnp.einsum(
                "nki,kij->nkj",
                normed[member],
                left_sets[member][layer_index],
                preferred_element_type=jnp.float32,
            ).astype(jnp.bfloat16)
            for member in range(2)
        ]
        permuted = (
            lax.all_to_all(first_out[0], "tensor", split_axis=2, concat_axis=1, tiled=True),
            lax.all_to_all(first_out[1], "tensor", split_axis=2, concat_axis=1, tiled=True),
        )
        permuted = [
            permuted[member].reshape(
                permuted[member].shape[0], all_blocks, local_blocks, fold_ratio
            )
            for member in range(2)
        ]
        right_quads = [
            right_sets[member][layer_index].reshape(
                local_blocks, fold_ratio, all_blocks, block_size
            )
            for member in range(2)
        ]
        mixture = [
            jnp.einsum(
                "nkmp,mpkl->nml",
                permuted[member],
                right_quads[member],
                preferred_element_type=jnp.float32,
            )
            for member in range(2)
        ]
        stored.append((residuals, factors, normed, permuted, mixture, right_quads, gain_pair))
        residuals = [residuals[member] + gelu_value(mixture[member]) for member in range(2)]
    final_gains = [gain_sets[0][layer_count], gain_sets[1][layer_count]]
    factors, outputs = norm_pair(residuals, final_gains, model_width)
    gradients = norm_back_pair(
        residuals,
        factors,
        final_gains,
        [outputs[member] - targets[member] for member in range(2)],
        [jnp.zeros_like(residuals[member]) for member in range(2)],
        model_width,
    )
    left_terms = []
    right_terms = []
    for layer_index in range(layer_count - 1, -1, -1):
        inputs, factors, normed, permuted, mixture, right_quads, gain_pair = stored[layer_index]
        slopes = [
            (gradients[member] * gelu_slope(mixture[member])).astype(jnp.bfloat16)
            for member in range(2)
        ]
        right_grad = [
            jnp.einsum(
                "nkmp,nml->mpkl",
                permuted[member],
                slopes[member],
                preferred_element_type=jnp.float32,
            ).reshape(local_blocks, block_size, block_size)
            for member in range(2)
        ]
        back_moved = [
            jnp.einsum(
                "nml,mpkl->nkmp",
                slopes[member],
                right_quads[member],
                preferred_element_type=jnp.float32,
            )
            .astype(jnp.bfloat16)
            .reshape(slopes[member].shape[0], all_blocks, local_blocks * fold_ratio)
            for member in range(2)
        ]
        arrived = (
            lax.all_to_all(back_moved[0], "tensor", split_axis=1, concat_axis=2, tiled=True),
            lax.all_to_all(back_moved[1], "tensor", split_axis=1, concat_axis=2, tiled=True),
        )
        left_grad = [
            jnp.einsum(
                "nki,nkj->kij", normed[member], arrived[member], preferred_element_type=jnp.float32
            )
            for member in range(2)
        ]
        grad_normed = [
            jnp.einsum(
                "nkj,kij->nki",
                arrived[member],
                left_sets[member][layer_index],
                preferred_element_type=jnp.float32,
            )
            for member in range(2)
        ]
        gradients = norm_back_pair(inputs, factors, gain_pair, grad_normed, gradients, model_width)
        layer_left = (left_grad[0] + left_grad[1])[None]
        layer_right = (right_grad[0] + right_grad[1])[None]
        layer_left, layer_right = (
            lax.psum(layer_left.astype(jnp.bfloat16), "dp").astype(jnp.float32),
            lax.psum(layer_right.astype(jnp.bfloat16), "dp").astype(jnp.float32),
        )
        left_terms.insert(0, layer_left)
        right_terms.insert(0, layer_right)
    left_stack = jnp.stack(left_terms)
    right_stack = jnp.stack(right_terms)
    left_total = left_stack[:, 0]
    right_total = right_stack[:, 0]
    grad_factor = 1.0 / math.sqrt(2 * tok_rows * sections * replicas)
    returned = [
        gradients[member].astype(jnp.bfloat16).reshape(sections, -1, local_blocks, block_size)
        for member in range(2)
    ]
    back_lead, back_trail = (
        lax.all_to_all(returned[0], "section", split_axis=0, concat_axis=0, tiled=True),
        lax.all_to_all(returned[1], "section", split_axis=0, concat_axis=0, tiled=True),
    )
    gathered = jnp.concatenate((back_lead, back_trail), axis=1).reshape(
        slot_total, local_blocks, block_size
    )
    combined = (
        gathered[chosen[:, 0]].astype(jnp.float32) + gathered[chosen[:, 1]].astype(jnp.float32)
    ) * 0.5
    d_patches = combined.astype(jnp.bfloat16).reshape(tok_rows, feat_local)
    return (d_patches, (left_total * grad_factor)[None], (right_total * grad_factor)[None])


def solution(mesh):
    in_specs = (
        P(("section", "dp"), "tensor"),
        P(("section", "dp"), "tensor"),
        P(("section", "dp"), None),
        P("section", None, "tensor", None, None),
        P("section", None, "tensor", None, None),
        P("section", None, "tensor"),
    )
    out_specs = (
        P(("section", "dp"), "tensor"),
        P("section", None, "tensor", None, None),
        P("section", None, "tensor", None, None),
    )
    return jax.shard_map(shards, mesh=mesh, in_specs=in_specs, out_specs=out_specs, check_vma=False)
```

profile of v0, /device:TPU:1, one launch (start us, length us, event | category | flops | bytes accessed | tf_op | source)
XLA Modules:
  0.0 724.6 jit_solution(267021291484464371)
XLA Ops:
  10.0 3.7 gather_fusion.4
  22.7 5.0 all-to-all-start
  27.7 8.3 %all-to-all-done = bf16[4,128,4,128]{3,1,2,0:T(8,128)(2,1)S(1)} async-done(((bf16[4,128,4,128]{3,1,2,0:T(8,128)(2,1)}), bf16[4,128,4,128]{3,1,2,0:T(8,128)(2,1)S(1)}, u32[]{:S(2)}, u32[]{:S(2)}) %all-to-all-start) | async-done | bytes 524320 | tf_op jit(solution)/shard_map/all_to_all | solution.py:98
  36.3 34.7 %all-reduce.10 = (f32[256]{0:T(256)S(1)}, f32[256]{0:T(256)S(1)}) all-reduce(f32[256]{0:T(256)S(1)} %reduce_sum.196, f32[256]{0:T(256)S(1)} %reduce_sum.185), channel_id=1, replica_groups=mesh['section'=4,'tensor'=16,'dp'=2] {'tensor'}, use_global_device_ids=true, to_apply=%region_24.25 | all-reduce | flops 512 | bytes 4096 | tf_op jit(solution)/shard_map/psum | solution.py:26
  74.4 3.5 all-to-all-start.1
  79.1 6.2 all-to-all-done.1
  85.2 3.5 all-to-all-start.11
  89.8 6.6 all-to-all-done.11
  99.0 29.5 %all-reduce.9 = (f32[256]{0:T(256)S(1)}, f32[256]{0:T(256)S(1)}) all-reduce(f32[256]{0:T(256)S(1)} %get-tuple-element.57, f32[256]{0:T(256)S(1)} %get-tuple-element.55), channel_id=1, replica_groups=mesh['section'=4,'tensor'=16,'dp'=2] {'tensor'}, use_global_device_ids=true, to_apply=%region_26.27 | all-reduce | flops 512 | bytes 4096 | tf_op jit(solution)/shard_map/psum | solution.py:26
  130.2 3.5 all-to-all-start.2
  134.9 6.1 all-to-all-done.2
  141.1 3.5 all-to-all-start.12
  145.6 6.3 all-to-all-done.12
  154.4 29.5 %all-reduce.8 = (f32[256]{0:T(256)S(1)}, f32[256]{0:T(256)S(1)}) all-reduce(f32[256]{0:T(256)S(1)} %get-tuple-element.53, f32[256]{0:T(256)S(1)} %get-tuple-element.51), channel_id=1, replica_groups=mesh['section'=4,'tensor'=16,'dp'=2] {'tensor'}, use_global_device_ids=true, to_apply=%region_28.29 | all-reduce | flops 512 | bytes 4096 | tf_op jit(solution)/shard_map/psum | solution.py:26
  185.7 3.7 all-to-all-start.3
  192.2 4.3 all-to-all-done.3
  197.2 3.5 all-to-all-start.13
  203.3 4.8 all-to-all-done.13
  208.1 4.1 all-to-all-start.5
  216.4 30.1 %all-reduce.7 = (f32[256]{0:T(256)S(1)}, f32[256]{0:T(256)S(1)}) all-reduce(f32[256]{0:T(256)S(1)} %get-tuple-element.49, f32[256]{0:T(256)S(1)} %get-tuple-element.47), channel_id=1, replica_groups=mesh['section'=4,'tensor'=16,'dp'=2] {'tensor'}, use_global_device_ids=true, to_apply=%region_30.31 | all-reduce | flops 512 | bytes 4096 | tf_op jit(solution)/shard_map/psum | solution.py:26
  250.8 4.2 all-to-all-start.4
  258.7 3.7 all-to-all-done.4
  262.4 4.2 all-to-all-start.14
  280.8 33.1 %all-reduce.6 = (f32[256]{0:T(256)S(1)}, f32[256]{0:T(256)S(1)}) all-reduce(f32[256]{0:T(256)S(1)} %get-tuple-element.90, f32[256]{0:T(256)S(1)} %get-tuple-element.92), channel_id=1, replica_groups=mesh['section'=4,'tensor'=16,'dp'=2] {'tensor'}, use_global_device_ids=true, to_apply=%region_12.13 | all-reduce | flops 512 | bytes 4096 | tf_op jit(solution)/shard_map/psum | solution.py:26
  316.1 29.1 %all-reduce.5 = (f32[256]{0:T(256)}, f32[256]{0:T(256)}) all-reduce(f32[256]{0:T(256)S(1)} %get-tuple-element.6, f32[256]{0:T(256)S(1)} %get-tuple-element.5), channel_id=1, replica_groups=mesh['section'=4,'tensor'=16,'dp'=2] {'tensor'}, use_global_device_ids=true, to_apply=%region_34.35 | all-reduce | flops 512 | bytes 4096 | tf_op jit(solution)/shard_map/psum | solution.py:43
  352.4 4.2 all-to-all-start.6
  358.6 5.3 all-to-all-done.6
  363.9 4.2 all-to-all-start.15
  377.5 30.4 %all-reduce.4 = (f32[256]{0:T(256)}, f32[256]{0:T(256)}) all-reduce(f32[256]{0:T(256)S(1)} %get-tuple-element.94, f32[256]{0:T(256)S(1)} %get-tuple-element.96), channel_id=1, replica_groups=mesh['section'=4,'tensor'=16,'dp'=2] {'tensor'}, use_global_device_ids=true, to_apply=%region_36.37 | all-reduce | flops 512 | bytes 4096 | tf_op jit(solution)/shard_map/psum | solution.py:43
  410.0 3.9 fusion.45
  419.8 4.3 all-to-all-start.7
  426.1 5.4 all-to-all-done.7
  431.5 3.8 all-to-all-start.16
  443.6 29.9 %all-reduce.3 = (f32[256]{0:T(256)S(1)}, f32[256]{0:T(256)S(1)}) all-reduce(f32[256]{0:T(256)S(1)} %get-tuple-element.98, f32[256]{0:T(256)S(1)} %get-tuple-element.100), channel_id=1, replica_groups=mesh['section'=4,'tensor'=16,'dp'=2] {'tensor'}, use_global_device_ids=true, to_apply=%region_38.39 | all-reduce | flops 512 | bytes 4096 | tf_op jit(solution)/shard_map/psum | solution.py:43
  483.5 3.7 all-to-all-start.8
  488.1 7.1 all-to-all-done.8
  495.2 3.5 all-to-all-start.17
  500.9 5.5 all-to-all-done.17
  507.5 29.5 %all-reduce.2 = (f32[256]{0:T(256)S(1)}, f32[256]{0:T(256)S(1)}) all-reduce(f32[256]{0:T(256)S(1)} %get-tuple-element.102, f32[256]{0:T(256)S(1)} %get-tuple-element.104), channel_id=1, replica_groups=mesh['section'=4,'tensor'=16,'dp'=2] {'tensor'}, use_global_device_ids=true, to_apply=%region_40.41 | all-reduce | flops 512 | bytes 4096 | tf_op jit(solution)/shard_map/psum | solution.py:43
  545.7 3.7 all-to-all-start.9
  550.3 6.4 all-to-all-done.9
  556.7 3.5 all-to-all-start.18
  561.5 7.3 %all-to-all-done.18 = bf16[256,64,8]{0,2,1:T(8,128)(2,1)S(1)} async-done(((bf16[256,64,8]{0,2,1:T(8,128)(2,1)}), bf16[256,64,8]{0,2,1:T(8,128)(2,1)S(1)}, u32[]{:S(2)}, u32[]{:S(2)}) %all-to-all-start.18) | async-done | bytes 262176 | tf_op jit(solution)/shard_map/all_to_all | solution.py:197
  570.8 30.1 %all-reduce.1 = (f32[256]{0:T(256)S(1)}, f32[256]{0:T(256)S(1)}) all-reduce(f32[256]{0:T(256)S(1)} %get-tuple-element.106, f32[256]{0:T(256)S(1)} %get-tuple-element.108), channel_id=1, replica_groups=mesh['section'=4,'tensor'=16,'dp'=2] {'tensor'}, use_global_device_ids=true, to_apply=%region_42.43 | all-reduce | flops 512 | bytes 4096 | tf_op jit(solution)/shard_map/psum | solution.py:43
  603.7 4.8 all-to-all-start.19
  609.3 4.6 all-to-all-done.19
  618.7 4.2 all-to-all-done.10
  625.9 88.9 %all-reduce.14.cloned.1.call-done = (bf16[1,1,4,128,128]{4,3,2,1,0:T(8,128)(2,1)}, bf16[1,1,4,128,128]{4,3,2,1,0:T(8,128)(2,1)}, bf16[1,1,4,128,128]{4,3,2,1,0:T...) async-done(((bf16[1,1,4,128,128]{4,3,2,1,0:T(8,128)(2,1)}, ...) | async-done | bytes 1048592 | tf_op jit(solution)/shard_map/psum | solution.py:218
  (328 shorter events, 140.5 us)
Async XLA Ops:
  7.2 10.2 %copy-start = (bf16[192,512]{1,0:T(8,128)(2,1)S(1)}, bf16[192,512]{1,0:T(8,128)(2,1)}, u32[]{:S(2)}) copy-start(bf16[192,512]{1,0:T(8,128)(2,1)} %param.7) | copy-start | bytes 589828
  22.7 5.0 copy-start.54
  22.7 13.3 %all-to-all-start = ((bf16[4,128,4,128]{3,1,2,0:T(8,128)(2,1)}), bf16[4,128,4,128]{3,1,2,0:T(8,128)(2,1)S(1)}, u32[]{:S(2)}, u32[]{:S(2)}) async-start(bf16[4,128,4,128]{3,1,2,0:T(8,128)(2,1)} %get-tuple-element.83), calls=%async_computation | async-start | bytes 1048576 | tf_op jit(solution)/shard_map/all_to_all | solution.py:98
  71.7 26.1 %copy-start.2 = (f32[4,64,4,128]{3,1,0,2:T(8,128)}, f32[4,64,4,128]{3,1,0,2:T(8,128)S(1)}, u32[]{:S(2)}) copy-start(f32[4,64,4,128]{3,1,0,2:T(8,128)S(1)} %copy.239) | copy-start | bytes 1572868
  71.8 25.0 %copy-start.4 = (f32[4,64,4,128]{3,1,0,2:T(8,128)}, f32[4,64,4,128]{3,1,0,2:T(8,128)S(1)}, u32[]{:S(2)}) copy-start(f32[4,64,4,128]{3,1,0,2:T(8,128)S(1)} %copy.267) | copy-start | bytes 1572868
  72.0 5.9 copy-start.26
  74.4 10.8 %all-to-all-start.1 = ((bf16[256,4,128]{0,1,2:T(4,128)(2,1)}), bf16[256,4,128]{0,1,2:T(4,128)(2,1)S(1)}, u32[]{:S(2)}, u32[]{:S(2)}) async-start(bf16[256,4,128]{0,1,2:T(4,128)(2,1)} %copy.240), calls=%async_computation.1 | async-start | bytes 524288 | tf_op jit(solution)/shard_map/all_to_all | solution.py:131
  79.1 9.7 %copy-start.52 = (bf16[1,4,4,128,128]{4,3,2,1,0:T(8,128)(2,1)S(1)}, bf16[1,4,4,128,128]{4,3,2,1,0:T(8,128)(2,1)}, u32[]{:S(2)}) copy-start(bf16[1,4,4,128,128]{4,3,2,1,0:T(8,128)(2,1)} %param.10) | copy-start | bytes 1572868
  85.2 11.2 %all-to-all-start.11 = ((bf16[256,4,128]{0,1,2:T(4,128)(2,1)}), bf16[256,4,128]{0,1,2:T(4,128)(2,1)S(1)}, u32[]{:S(2)}, u32[]{:S(2)}) async-start(bf16[256,4,128]{0,1,2:T(4,128)(2,1)} %copy.268), calls=%async_computation.11 | async-start | bytes 524288 | tf_op jit(solution)/shard_map/all_to_all | solution.py:132
  89.5 63.8 %copy-start.8 = (bf16[1,1,4,128,128]{4,3,2,1,0:T(8,128)(2,1)}, bf16[1,1,4,128,128]{4,3,2,1,0:T(8,128)(2,1)S(1)}, u32[]{:S(2)}) copy-start(bf16[1,1,4,128,128]{4,3,2,1,0:T(8,128)(2,1)S(1)} %get-tuple-element.62) | copy-start | bytes 393220
  89.5 123.1 %copy-start.10 = (bf16[1,1,4,128,128]{4,3,2,1,0:T(8,128)(2,1)}, bf16[1,1,4,128,128]{4,3,2,1,0:T(8,128)(2,1)S(1)}, u32[]{:S(2)}) copy-start(bf16[1,1,4,128,128]{4,3,2,1,0:T(8,128)(2,1)S(1)} %get-tuple-element.64) | copy-start | bytes 393220
  89.8 8.1 %copy-start.14 = (bf16[256,64,4,2]{0,1,3,2:T(8,128)(2,1)}, bf16[256,64,4,2]{0,1,3,2:T(8,128)(2,1)S(1)}, u32[]{:S(2)}) copy-start(bf16[256,64,4,2]{0,1,3,2:T(8,128)(2,1)S(1)} %reshape.358) | copy-start | bytes 786436
  130.2 10.8 %all-to-all-start.2 = ((bf16[256,4,128]{0,1,2:T(4,128)(2,1)}), bf16[256,4,128]{0,1,2:T(4,128)(2,1)S(1)}, u32[]{:S(2)}, u32[]{:S(2)}) async-start(bf16[256,4,128]{0,1,2:T(4,128)(2,1)} %copy.243), calls=%async_computation.2 | async-start | bytes 524288 | tf_op jit(solution)/shard_map/all_to_all | solution.py:131
  141.1 10.8 %all-to-all-start.12 = ((bf16[256,4,128]{0,1,2:T(4,128)(2,1)}), bf16[256,4,128]{0,1,2:T(4,128)(2,1)S(1)}, u32[]{:S(2)}, u32[]{:S(2)}) async-start(bf16[256,4,128]{0,1,2:T(4,128)(2,1)} %copy.271), calls=%async_computation.12 | async-start | bytes 524288 | tf_op jit(solution)/shard_map/all_to_all | solution.py:132
  185.7 10.8 %all-to-all-start.3 = ((bf16[256,4,128]{0,1,2:T(4,128)(2,1)}), bf16[256,4,128]{0,1,2:T(4,128)(2,1)S(1)}, u32[]{:S(2)}, u32[]{:S(2)}) async-start(bf16[256,4,128]{0,1,2:T(4,128)(2,1)} %copy.246), calls=%async_computation.3 | async-start | bytes 524288 | tf_op jit(solution)/shard_map/all_to_all | solution.py:131
  197.2 10.9 %all-to-all-start.13 = ((bf16[256,4,128]{0,1,2:T(4,128)(2,1)}), bf16[256,4,128]{0,1,2:T(4,128)(2,1)S(1)}, u32[]{:S(2)}, u32[]{:S(2)}) async-start(bf16[256,4,128]{0,1,2:T(4,128)(2,1)} %copy.274), calls=%async_computation.13 | async-start | bytes 524288 | tf_op jit(solution)/shard_map/all_to_all | solution.py:132
  208.1 42.7 %all-to-all-start.5 = ((bf16[4,128,4,128]{3,1,2,0:T(8,128)(2,1)}), bf16[4,128,4,128]{3,1,2,0:T(8,128)(2,1)}, u32[]{:S(2)}, u32[]{:S(2)}) async-start(bf16[4,128,4,128]{3,1,2,0:T(8,128)(2,1)} %get-tuple-element.82), calls=%async_computation.5 | async-start | bytes 1048576 | tf_op jit(solution)/shard_map/all_to_all | solution.py:99
  246.5 4.3 copy-start.63
  250.8 11.6 %all-to-all-start.4 = ((bf16[256,4,128]{0,1,2:T(4,128)(2,1)}), bf16[256,4,128]{0,1,2:T(4,128)(2,1)}, u32[]{:S(2)}, u32[]{:S(2)}) async-start(bf16[256,4,128]{0,1,2:T(4,128)(2,1)} %copy.249), calls=%async_computation.4 | async-start | bytes 524288 | tf_op jit(solution)/shard_map/all_to_all | solution.py:131
  262.4 11.5 %all-to-all-start.14 = ((bf16[256,4,128]{0,1,2:T(4,128)(2,1)}), bf16[256,4,128]{0,1,2:T(4,128)(2,1)}, u32[]{:S(2)}, u32[]{:S(2)}) async-start(bf16[256,4,128]{0,1,2:T(4,128)(2,1)} %copy.277), calls=%async_computation.14 | async-start | bytes 524288 | tf_op jit(solution)/shard_map/all_to_all | solution.py:132
  346.6 2.6 copy-start.47
  352.4 11.5 %all-to-all-start.6 = ((bf16[256,64,8]{0,2,1:T(8,128)(2,1)}), bf16[256,64,8]{0,2,1:T(8,128)(2,1)}, u32[]{:S(2)}, u32[]{:S(2)}) async-start(bf16[256,64,8]{0,2,1:T(8,128)(2,1)} %copy.254), calls=%async_computation.6 | async-start | bytes 524288 | tf_op jit(solution)/shard_map/all_to_all | solution.py:196
  363.9 11.5 %all-to-all-start.15 = ((bf16[256,64,8]{0,2,1:T(8,128)(2,1)}), bf16[256,64,8]{0,2,1:T(8,128)(2,1)}, u32[]{:S(2)}, u32[]{:S(2)}) async-start(bf16[256,64,8]{0,2,1:T(8,128)(2,1)} %copy.281), calls=%async_computation.15 | async-start | bytes 524288 | tf_op jit(solution)/shard_map/all_to_all | solution.py:197
  410.0 3.9 copy-start.23
  413.9 3.9 copy-start.24
  419.8 4.3 copy-start.21
  419.8 4.3 copy-start.25
  419.8 11.7 %all-to-all-start.7 = ((bf16[256,64,8]{0,2,1:T(8,128)(2,1)}), bf16[256,64,8]{0,2,1:T(8,128)(2,1)}, u32[]{:S(2)}, u32[]{:S(2)}) async-start(bf16[256,64,8]{0,2,1:T(8,128)(2,1)} %copy.257), calls=%async_computation.7 | async-start | bytes 524288 | tf_op jit(solution)/shard_map/all_to_all | solution.py:196
  424.1 11.1 %copy-start.7 = (bf16[1,4,4,128,128]{4,3,2,1,0:T(8,128)(2,1)S(1)}, bf16[1,4,4,128,128]{4,3,2,1,0:T(8,128)(2,1)}, u32[]{:S(2)}) copy-start(bf16[1,4,4,128,128]{4,3,2,1,0:T(8,128)(2,1)} %param.9) | copy-start | bytes 1572868
  431.5 11.1 %all-to-all-start.16 = ((bf16[256,64,8]{0,2,1:T(8,128)(2,1)}), bf16[256,64,8]{0,2,1:T(8,128)(2,1)S(1)}, u32[]{:S(2)}, u32[]{:S(2)}) async-start(bf16[256,64,8]{0,2,1:T(8,128)(2,1)} %copy.284), calls=%async_computation.16 | async-start | bytes 524288 | tf_op jit(solution)/shard_map/all_to_all | solution.py:197
  474.2 2.6 copy-start.19
  477.7 2.7 copy-start.39
  483.5 3.7 copy-start.17
  483.5 11.7 %all-to-all-start.8 = ((bf16[256,64,8]{0,2,1:T(8,128)(2,1)}), bf16[256,64,8]{0,2,1:T(8,128)(2,1)S(1)}, u32[]{:S(2)}, u32[]{:S(2)}) async-start(bf16[256,64,8]{0,2,1:T(8,128)(2,1)} %copy.260), calls=%async_computation.8 | async-start | bytes 524288 | tf_op jit(solution)/shard_map/all_to_all | solution.py:196
  495.2 11.2 %all-to-all-start.17 = ((bf16[256,64,8]{0,2,1:T(8,128)(2,1)}), bf16[256,64,8]{0,2,1:T(8,128)(2,1)S(1)}, u32[]{:S(2)}, u32[]{:S(2)}) async-start(bf16[256,64,8]{0,2,1:T(8,128)(2,1)} %copy.287), calls=%async_computation.17 | async-start | bytes 524288 | tf_op jit(solution)/shard_map/all_to_all | solution.py:197
  506.4 31.3 %copy-start.34 = (f32[256,4,128]{2,0,1:T(8,128)S(1)}, f32[256,4,128]{2,0,1:T(8,128)}, u32[]{:S(2)}) copy-start(f32[256,4,128]{2,0,1:T(8,128)} %get-tuple-element.85) | copy-start | bytes 1572868
  537.7 2.5 copy-start.15
  545.7 3.7 copy-start.13
  545.7 3.7 copy-start.45
  545.7 11.0 %all-to-all-start.9 = ((bf16[256,64,8]{0,2,1:T(8,128)(2,1)}), bf16[256,64,8]{0,2,1:T(8,128)(2,1)S(1)}, u32[]{:S(2)}, u32[]{:S(2)}) async-start(bf16[256,64,8]{0,2,1:T(8,128)(2,1)} %copy.263), calls=%async_computation.9 | async-start | bytes 524288 | tf_op jit(solution)/shard_map/all_to_all | solution.py:196
  549.4 10.9 %copy-start.3 = (f32[4,64,4,128]{3,1,0,2:T(8,128)S(1)}, f32[4,64,4,128]{3,1,0,2:T(8,128)}, u32[]{:S(2)}) copy-start(f32[4,64,4,128]{3,1,0,2:T(8,128)} %copy-done.2) | copy-start | bytes 1572868
  556.7 12.1 %all-to-all-start.18 = ((bf16[256,64,8]{0,2,1:T(8,128)(2,1)}), bf16[256,64,8]{0,2,1:T(8,128)(2,1)S(1)}, u32[]{:S(2)}, u32[]{:S(2)}) async-start(bf16[256,64,8]{0,2,1:T(8,128)(2,1)} %copy.290), calls=%async_computation.18 | async-start | bytes 524288 | tf_op jit(solution)/shard_map/all_to_all | solution.py:197
  560.2 154.6 %all-reduce.14.cloned.1.call-start = ((), (), s32[]{:S(2)}) async-start(), calls=%async_computation.20 | async-start | bytes 2097152 | tf_op jit(solution)/shard_map/psum | solution.py:218
  561.2 7.5 %copy-start.5 = (f32[4,64,4,128]{3,1,0,2:T(8,128)S(1)}, f32[4,64,4,128]{3,1,0,2:T(8,128)}, u32[]{:S(2)}) copy-start(f32[4,64,4,128]{3,1,0,2:T(8,128)} %copy-done.4) | copy-start | bytes 1572868
  568.8 32.1 %copy-start.70 = (f32[256]{0:T(256)S(1)}, f32[256]{0:T(256)}, u32[]{:S(2)}) copy-start(f32[256]{0:T(256)} %copy-done.69) | copy-start | bytes 3076
  603.0 5.5 copy-start.40
  603.7 10.3 %all-to-all-start.19 = ((bf16[4,64,4,128]{3,1,2,0:T(8,128)(2,1)}), bf16[4,64,4,128]{3,1,2,0:T(8,128)(2,1)S(1)}, u32[]{:S(2)}, u32[]{:S(2)}) async-start(bf16[4,64,4,128]{3,1,2,0:T(8,128)(2,1)} %copy.293), calls=%async_computation.19 | async-start | bytes 524288 | tf_op jit(solution)/shard_map/all_to_all | solution.py:234
  614.0 8.9 %all-to-all-start.10 = ((bf16[4,64,4,128]{3,1,2,0:T(8,128)(2,1)}), bf16[4,64,4,128]{3,1,2,0:T(8,128)(2,1)S(1)}, u32[]{:S(2)}, u32[]{:S(2)}) async-start(bf16[4,64,4,128]{3,1,2,0:T(8,128)(2,1)} %copy.266), calls=%async_computation.10 | async-start | bytes 524288 | tf_op jit(solution)/shard_map/all_to_all | solution.py:233
  (47 other events, 47.5 us)
Sparse Core Ops, SparseCore 0:
  601.7 113.0 all-reduce.13
where the time goes:
time: 731 us; the launch traced here: 725 us
  blocking collectives  306 us (42%)
  waiting for transfers between devices  188 us (26%)
  starting transfers between devices  77.9 us (11%)
  local copies, waits for them, and re-layouts  63 us (9%)
  matrix products  48.4 us (7%)
  other arithmetic  25.9 us (4%)
  between operations  15.1 us (2%)
    psum x5, blocking collectives, norm_pair(): lax.psum((jnp.sum(residuals[0] * residuals[0], axis=(1, 2)), jnp.sum(resi...  157 us
    psum x5, blocking collectives, norm_back_pair(): lax.psum((jnp.sum(weighted[0] * residuals[0], axis=(1, 2)), jnp.sum(weigh...  149 us
    psum x1, waiting for transfers between devices, shards(): lax.psum(layer_left.astype(jnp.bfloat16), 'dp').astype(jnp.float32)  88.9 us
    all_to_all x4, waiting for transfers between devices, shards(): lax.all_to_all(back_moved[0], 'tensor', split_axis=1, concat_axis=2, tile...  24.2 us
    all_to_all x4, waiting for transfers between devices, shards(): lax.all_to_all(first_out[0], 'tensor', split_axis=2, concat_axis=1, tiled...  20.2 us
    all_to_all x4, waiting for transfers between devices, shards(): lax.all_to_all(back_moved[1], 'tensor', split_axis=1, concat_axis=2, tile...  19.3 us
    all_to_all x4, waiting for transfers between devices, shards(): lax.all_to_all(first_out[1], 'tensor', split_axis=2, concat_axis=1, tiled...  18.6 us
    unnamed x150, local copies, waits for them, and re-layouts  16.6 us
  transfers between devices with their start and end apart: 21, of which 20 were waited for; matrix products, arithmetic and copies ran while one was open for 7% of the time, Pallas kernels for 0%

commit v1 on v0

v1 whole, which is shorter than its diff:
```python
import functools
import math

import jax
import jax.numpy as jnp
from jax import lax
from jax.experimental import pallas as pl
from jax.experimental.pallas import tpu as pltpu
from jax.sharding import PartitionSpec as P

EPSILON = 1e-06
TANH_SLOPE = 0.7978845608028654
CUBIC_TERM = 0.044715
MESH = pl.DeviceIdType.MESH
LANES = 128
CHUNKS = 3
F32 = jnp.float32
BF16 = jnp.bfloat16


def gelu_both(v):
    square = v * v
    tangent = jnp.tanh(TANH_SLOPE * (v + CUBIC_TERM * square * v))
    half = 0.5 + 0.5 * tangent
    slope = half + v * half * (1.0 - tangent) * (TANH_SLOPE + 3.0 * CUBIC_TERM * TANH_SLOPE * square)
    return v * half, slope


def dot(a, b, dims):
    return lax.dot_general(a, b, (dims, ((), ())), preferred_element_type=F32)


NN = ((1,), (0,))
TN = ((0,), (0,))
NT = ((1,), (1,))


def kernel(
    width,
    layers,
    blocks,
    total_tokens,
    patches,
    teacher,
    pairs,
    left,
    right,
    gains_in,
    d_out,
    gl_out,
    gr_out,
    raw_p,
    raw_t,
    raw_i,
    wbuf,
    graw,
    gpad,
    gains,
    perm,
    perm_t,
    hot,
    hbuf,
    hg,
    zn,
    bbuf,
    slope,
    sbuf,
    gbuf,
    tbuf,
    gb16,
    ga16,
    amsg,
    zrecv,
    st_s,
    st_r,
    fst_s,
    fst_r,
    gacc,
    gsend,
    grecv,
    fin,
    d_s,
    d_r,
    m_s,
    m_r,
    t_s,
    t_r,
    f_s,
    f_r,
    w_s,
    w_r,
    n_s,
    n_r,
    raw_s,
    raw_r,
    g_s,
    g_r,
    o_l,
    o_s,
    o_r,
    e_s,
    e_r,
):
    x = lax.axis_index("section")
    t = lax.axis_index("tensor")
    d = lax.axis_index("dp")
    sections = 4
    tok = patches.shape[0]
    bs = LANES
    feat = blocks * bs
    model = feat * width
    all_blocks = blocks * width
    rows = bs // width
    fold = bs // all_blocks
    partner = {"dp": 1 - d}

    barrier = pltpu.get_barrier_semaphore()

    def greet(i, _):
        pl.semaphore_signal(
            barrier, inc=1, device_id={"tensor": lax.rem(t + i, width)}, device_id_type=MESH
        )
        return 0

    lax.fori_loop(1, width, greet, 0)
    pl.semaphore_signal(barrier, inc=1, device_id=partner, device_id_type=MESH)
    for dx in range(1, sections):
        for e in range(2):
            pl.semaphore_signal(
                barrier,
                inc=1,
                device_id={"section": lax.rem(x + dx, sections), "dp": e},
                device_id_type=MESH,
            )

    def column_of(r):
        m = r >> 7
        w = r & (bs - 1)
        q = w >> (all_blocks.bit_length() - 1)
        k = w & (all_blocks - 1)
        return k * rows + m * fold + q

    def fill_perm(i, _):
        base = i * bs
        r = lax.broadcasted_iota(jnp.int32, (bs, feat), 0) + base
        c = lax.broadcasted_iota(jnp.int32, (bs, feat), 1)
        perm[pl.ds(base, bs), :] = jnp.where(column_of(r) == c, 1.0, 0.0).astype(BF16)
        perm_t[pl.ds(base, bs), :] = jnp.where(column_of(c) == r, 1.0, 0.0).astype(BF16)
        return 0

    lax.fori_loop(0, blocks, fill_perm, 0)
    gpad[...] = jnp.zeros_like(gpad)
    gacc[...] = jnp.zeros_like(gacc)

    lower = jnp.where(
        lax.broadcasted_iota(jnp.int32, (tok, tok), 0)
        > lax.broadcasted_iota(jnp.int32, (tok, tok), 1),
        1.0,
        0.0,
    ).astype(BF16)
    lane = lax.broadcasted_iota(jnp.int32, (tok, LANES), 1)

    def one_hot(ids, critic, offset):
        named = jnp.where((ids[:, 0:1] == critic) | (ids[:, 1:2] == critic), 1.0, 0.0)
        named = jnp.broadcast_to(named, (tok, LANES))
        rank = dot(lower, named.astype(BF16), NN)
        at = lane.astype(F32) - offset
        return jnp.where((rank == at) & (named > 0.5), 1.0, 0.0).astype(BF16)

    own_ids = pairs[...]
    hot[0] = one_hot(own_ids, d, 0.0)
    hot[2] = one_hot(own_ids, d + 2, 0.0)
    hbuf[0, 0] = dot(patches[...], hot[0], TN)
    tbuf[0] = dot(teacher[...], hot[0], TN).astype(BF16)

    pl.semaphore_wait(barrier, (width - 1) + 1 + 2 * (sections - 1))

    raws = ((pairs, raw_i), (patches, raw_p), (teacher, raw_t))
    for at, (src, dst) in enumerate(raws):
        pltpu.make_async_remote_copy(
            src_ref=src,
            dst_ref=dst,
            send_sem=raw_s.at[at],
            recv_sem=raw_r.at[at],
            device_id=partner,
            device_id_type=MESH,
        ).start()

    slot_here = x // 2
    runs_here = lax.rem(x, 2) == d
    half = pl.ds(2 * d, 2)
    lane_half = pl.ds(pl.multiple_of(d * (feat // 2), LANES), feat // 2)
    for dx in range(1, sections):
        pltpu.make_async_remote_copy(
            src_ref=gains_in.at[:, lane_half],
            dst_ref=graw.at[slot_here, :, lane_half],
            send_sem=n_s.at[dx - 1],
            recv_sem=n_r.at[slot_here],
            device_id={"section": lax.rem(x + dx, sections), "dp": lax.rem(x, 2)},
            device_id_type=MESH,
        ).start()

    def send_factors(layer, _):
        for f, src in enumerate((left, right)):
            for dx in (2, 1, 3):
                pltpu.make_async_remote_copy(
                    src_ref=src.at[layer, half],
                    dst_ref=wbuf.at[slot_here, layer, f, half],
                    send_sem=w_s,
                    recv_sem=w_r.at[slot_here, layer, f],
                    device_id={"section": lax.rem(x + dx, sections), "dp": lax.rem(x, 2)},
                    device_id_type=MESH,
                ).start()
        return 0

    lax.fori_loop(0, layers, send_factors, 0)

    @pl.when(runs_here)
    def _():
        pltpu.make_async_copy(gains_in, graw.at[slot_here], n_r.at[slot_here]).start()

        def take(layer, _):
            for f, src in enumerate((left, right)):
                pltpu.make_async_copy(
                    src.at[layer], wbuf.at[slot_here, layer, f], w_r.at[slot_here, layer, f]
                ).start()
            return 0

        lax.fori_loop(0, layers, take, 0)

    def await_bytes(ref, sem):
        pltpu.make_async_copy(ref, ref, sem).wait()

    def spread_gains(j):
        await_bytes(graw.at[j], n_r.at[j])
        gpad[j, 0 : layers + 1, :] = graw[j]

        def one(layer, _):
            pick = jnp.where(
                lax.broadcasted_iota(jnp.int32, (16, LANES), 0) == layer, 1.0, 0.0
            ).astype(BF16)
            gains[j, layer] = dot(gpad[j], pick, TN)
            return 0

        lax.fori_loop(0, layers + 1, one, 0)

    spread_gains(0)

    await_bytes(raw_i, raw_r.at[0])
    other_ids = raw_i[...]
    hot[1] = one_hot(other_ids, d, 0.0)
    hot[3] = one_hot(other_ids, d + 2, float(LANES // 2))
    await_bytes(raw_p, raw_r.at[1])
    hbuf[0, 1] = dot(raw_p[...], hot[1], TN)
    hbuf[0, 2] = dot(patches[...], hot[2], TN) + dot(raw_p[...], hot[3], TN)
    spread_gains(1)

    def exchange(step, q):
        def one(i, _):
            peer = lax.rem(t + i, width)
            pltpu.make_async_remote_copy(
                src_ref=st_s.at[step, q],
                dst_ref=st_r.at[step, q, t],
                send_sem=t_s.at[step, q],
                recv_sem=t_r.at[step, q],
                device_id={"tensor": peer},
                device_id_type=MESH,
            ).start()
            pltpu.make_async_remote_copy(
                src_ref=amsg.at[step, q, peer],
                dst_ref=zrecv.at[step, q, t],
                send_sem=m_s.at[step, q],
                recv_sem=m_r.at[step, q],
                device_id={"tensor": peer},
                device_id_type=MESH,
            ).start()
            return 0

        lax.fori_loop(1, width, one, 0)
        pltpu.make_async_copy(st_s.at[step, q], st_r.at[step, q, t], t_r.at[step, q]).start()
        pltpu.make_async_copy(amsg.at[step, q, t], zrecv.at[step, q, t], m_r.at[step, q]).start()

    def fwd_send(layer, q):
        j = q // 2

        @pl.when(q != 1)
        def _():
            await_bytes(wbuf.at[j, layer, 0], w_r.at[j, layer, 0])

        h = hbuf[layer, q]
        st_s[layer, q] = jnp.sum(h * h, axis=0, keepdims=True)
        hg[layer, q] = (h * gains[j, layer]).astype(BF16)
        outs = []
        for k in range(blocks):
            out = dot(wbuf[j, layer, 0, k], hg[layer, q, k * bs : (k + 1) * bs, :], TN)
            outs.append(out.reshape(width, 1, rows, LANES))
        message = jnp.concatenate(outs, axis=1).reshape(width, blocks * rows, LANES)
        amsg[layer, q] = message.astype(BF16)
        exchange(layer, q)

    def fwd_take(layer, q):
        j = q // 2

        @pl.when(q != 1)
        def _():
            await_bytes(wbuf.at[j, layer, 1], w_r.at[j, layer, 1])

        await_bytes(st_r.at[layer, q], t_r.at[layer, q])
        await_bytes(zrecv.at[layer, q], m_r.at[layer, q])
        squares = jnp.sum(st_r[layer, q], axis=0)
        s = lax.rsqrt(squares / model + EPSILON)
        sbuf[layer, q] = s
        zn[layer, q] = dot(perm[...], zrecv[layer, q].reshape(feat, LANES), NN).astype(BF16)
        for m in range(blocks):
            part = slice(m * bs, (m + 1) * bs)
            b = dot(wbuf[j, layer, 1, m], zn[layer, q, part, :], TN) * s
            bbuf[layer, q, part, :] = b
            value, steep = gelu_both(b)
            slope[layer, q, part, :] = steep
            hbuf[layer + 1, q, part, :] = hbuf[layer, q, part, :] + value

    def first(q, _):
        fwd_send(0, q)
        return 0

    lax.fori_loop(0, CHUNKS, first, 0)

    await_bytes(raw_t, raw_r.at[2])
    tbuf[1] = dot(raw_t[...], hot[1], TN).astype(BF16)
    tbuf[2] = (dot(teacher[...], hot[2], TN) + dot(raw_t[...], hot[3], TN)).astype(BF16)

    def forward(i, _):
        layer = i // CHUNKS
        q = lax.rem(i, CHUNKS)
        fwd_take(layer, q)
        fwd_send(layer + 1, q)
        return 0

    lax.fori_loop(0, CHUNKS * (layers - 1), forward, 0)

    def last(q, _):
        fwd_take(layers - 1, q)
        j = q // 2
        h = hbuf[layers, q]
        gh = gains[j, layers] * h
        fst_s[q, 0] = jnp.sum(h * h, axis=0, keepdims=True)
        fst_s[q, 1] = jnp.sum(gh * gh, axis=0, keepdims=True)
        fst_s[q, 2] = jnp.sum(gh * tbuf[q].astype(F32), axis=0, keepdims=True)

        def one(i, _):
            pltpu.make_async_remote_copy(
                src_ref=fst_s.at[q],
                dst_ref=fst_r.at[q, t],
                send_sem=f_s.at[q],
                recv_sem=f_r.at[q],
                device_id={"tensor": lax.rem(t + i, width)},
                device_id_type=MESH,
            ).start()
            return 0

        lax.fori_loop(1, width, one, 0)
        pltpu.make_async_copy(fst_s.at[q], fst_r.at[q, t], f_r.at[q]).start()
        return 0

    lax.fori_loop(0, CHUNKS, last, 0)

    def send_grad(layer, f, j):
        critic = d + 2 * j
        for e in range(2):
            piece = gsend.at[j, layer, f, pl.ds(2 * e, 2)]
            landing = grecv.at[layer, f, x]
            stays = (critic == x) & (d == e)

            @pl.when(stays)
            def _():
                pltpu.make_async_copy(piece, landing, g_r.at[layer, f]).start()

            @pl.when(jnp.logical_not(stays))
            def _():
                pltpu.make_async_remote_copy(
                    src_ref=piece,
                    dst_ref=landing,
                    send_sem=g_s.at[j, layer, f],
                    recv_sem=g_r.at[layer, f],
                    device_id={"section": critic, "dp": e},
                    device_id_type=MESH,
                ).start()

    def factor_grad(layer, f, q, lhs, rhs):
        j = q // 2
        for k in range(blocks):
            part = slice(k * bs, (k + 1) * bs)
            term = dot(lhs[layer, q, part, :], rhs[part, :], NT)
            term = term + jnp.where(q == 1, gacc[f, k], 0.0)
            gacc[f, k] = term
            gsend[j, layer, f, k] = term.astype(BF16)

        @pl.when(q != 0)
        def _():
            send_grad(layer, f, j)

    def bwd_send(layer, q):
        j = q // 2
        step = layers + layer
        gbs = gbuf[q] * slope[layer, q] * sbuf[layer, q]
        st_s[step, q] = jnp.sum(gbs * bbuf[layer, q], axis=0, keepdims=True)
        gb16[...] = gbs.astype(BF16)
        outs = []
        for m in range(blocks):
            out = dot(wbuf[j, layer, 1, m], gb16[m * bs : (m + 1) * bs, :], NN)
            outs.append(out.astype(BF16))
        moved = dot(perm_t[...], jnp.concatenate(outs, axis=0), NN)
        amsg[step, q] = moved.astype(BF16).reshape(width, blocks * rows, LANES)
        exchange(step, q)

    def bwd_take(layer, q):
        j = q // 2
        step = layers + layer
        await_bytes(st_r.at[step, q], t_r.at[step, q])
        await_bytes(zrecv.at[step, q], m_r.at[step, q])
        inner = jnp.sum(st_r[step, q], axis=0)
        coefficient = sbuf[layer, q] * inner / model
        arrived = zrecv[step, q].astype(F32).reshape(width, blocks, rows, LANES)
        for k in range(blocks):
            part = slice(k * bs, (k + 1) * bs)
            ga16[part, :] = arrived[:, k].reshape(bs, LANES).astype(BF16)
            gu = dot(wbuf[j, layer, 0, k], ga16[part, :], NN)
            gbuf[q, part, :] = (
                gbuf[q, part, :]
                + gu * gains[j, layer, part, :]
                - hbuf[layer, q, part, :] * coefficient
            )

    grad_factor = 1.0 / math.sqrt(2 * total_tokens)
    outs = (gl_out, gr_out)

    def finish(layer):
        for f in range(2):
            await_bytes(grecv.at[layer, f], g_r.at[layer, f])
            total = grecv[layer, f, 0].astype(F32)
            for source in range(1, sections):
                total = total + grecv[layer, f, source].astype(F32)
            fin[layer, f] = total * grad_factor
            pltpu.make_async_remote_copy(
                src_ref=fin.at[layer, f],
                dst_ref=outs[f].at[layer, half],
                send_sem=o_s,
                recv_sem=o_r,
                device_id=partner,
                device_id_type=MESH,
            ).start()
            pltpu.make_async_copy(fin.at[layer, f], outs[f].at[layer, half], o_l).start()

    def turn(q, _):
        j = q // 2
        await_bytes(fst_r.at[q], f_r.at[q])
        sums = jnp.sum(fst_r[q], axis=0)
        s = lax.rsqrt(sums[0] / model + EPSILON)
        coefficient = s * s * s * (s * sums[1] - sums[2]) / model
        h = hbuf[layers, q]
        gain = gains[j, layers]
        e = (h * s * gain - tbuf[q].astype(F32)) * gain
        gbuf[q] = s * e - h * coefficient
        bwd_send(layers - 1, q)
        factor_grad(layers - 1, 1, q, zn, gb16)
        return 0

    lax.fori_loop(0, CHUNKS, turn, 0)

    def backward(i, _):
        layer = layers - 1 - i // CHUNKS
        q = lax.rem(i, CHUNKS)
        bwd_take(layer, q)
        bwd_send(layer - 1, q)
        factor_grad(layer, 0, q, hg, ga16)
        factor_grad(layer - 1, 1, q, zn, gb16)

        @pl.when((q == CHUNKS - 1) & (layer < layers - 1))
        def _():
            finish(layer + 1)

        return 0

    lax.fori_loop(0, CHUNKS * (layers - 1), backward, 0)

    def ending(q, _):
        bwd_take(0, q)
        factor_grad(0, 0, q, hg, ga16)
        return 0

    lax.fori_loop(0, CHUNKS, ending, 0)

    lead_own = gbuf[0].astype(BF16)
    lead_other = gbuf[1].astype(BF16)
    trail = gbuf[2].astype(BF16)
    d_s[...] = (dot(hot[1], lead_other, NT) + dot(hot[3], trail, NT)).astype(BF16)
    back = pltpu.make_async_remote_copy(
        src_ref=d_s,
        dst_ref=d_r,
        send_sem=e_s,
        recv_sem=e_r,
        device_id=partner,
        device_id_type=MESH,
    )
    back.start()
    own = dot(hot[0], lead_own, NT) + dot(hot[2], trail, NT)
    finish(1)
    back.wait()
    d_out[...] = ((own + d_r[...].astype(F32)) * 0.5).astype(BF16)
    finish(0)

    def drain(step, _):
        def one(q, _):
            await_bytes(amsg.at[step, q, pl.ds(0, width - 1)], m_s.at[step, q])
            await_bytes(st_r.at[step, q, pl.ds(0, width - 1)], t_s.at[step, q])
            return 0

        return lax.fori_loop(0, CHUNKS, one, 0)

    lax.fori_loop(0, 2 * layers, drain, 0)

    def drain_final(q, _):
        await_bytes(fst_r.at[q, pl.ds(0, width - 1)], f_s.at[q])
        return 0

    lax.fori_loop(0, CHUNKS, drain_final, 0)
    for at, (src, dst) in enumerate(raws):
        await_bytes(src, raw_s.at[at])
    await_bytes(wbuf.at[:, pl.ds(0, 3)], w_s)
    for at in range(sections - 1):
        await_bytes(graw.at[0, :, pl.ds(0, feat // 2)], n_s.at[at])

    def drain_grad(layer, _):
        for j in range(2):
            for f in range(2):
                local = (d + 2 * j) == x

                @pl.when(local)
                def _():
                    await_bytes(gsend.at[j, layer, f, pl.ds(0, 2)], g_s.at[j, layer, f])

                @pl.when(jnp.logical_not(local))
                def _():
                    await_bytes(gsend.at[j, layer, f], g_s.at[j, layer, f])

        return 0

    lax.fori_loop(0, layers, drain_grad, 0)
    await_bytes(fin, o_l)
    await_bytes(fin, o_s)
    await_bytes(fin, o_r)


def shards(width, patches, teacher, critic_pairs, left_factors, right_factors, norm_gains):
    tok, feat = patches.shape
    layers, blocks, bs = left_factors.shape[1:4]
    rows = bs // width
    steps = 2 * layers
    total_tokens = tok * 8
    vmem = pl.BlockSpec(memory_space=pltpu.VMEM)
    anyspace = pl.BlockSpec(memory_space=pl.ANY)
    tile = (feat, LANES)
    message = (steps, CHUNKS, width, blocks * rows, LANES)
    dma = pltpu.SemaphoreType.DMA
    scratch = [
        pltpu.VMEM((tok, feat), BF16),
        pltpu.VMEM((tok, feat), BF16),
        pltpu.VMEM((tok, 2), jnp.int32),
        pltpu.VMEM((2, layers, 2, blocks, bs, bs), BF16),
        pltpu.VMEM((2, layers + 1, feat), BF16),
        pltpu.VMEM((2, 16, feat), BF16),
        pltpu.VMEM((2, layers + 1) + tile, F32),
        pltpu.VMEM((feat, feat), BF16),
        pltpu.VMEM((feat, feat), BF16),
        pltpu.VMEM((4, tok, LANES), BF16),
        pltpu.VMEM((layers + 1, CHUNKS) + tile, F32),
        pltpu.VMEM((layers, CHUNKS) + tile, BF16),
        pltpu.VMEM((layers, CHUNKS) + tile, BF16),
        pltpu.VMEM((layers, CHUNKS) + tile, F32),
        pltpu.VMEM((layers, CHUNKS) + tile, F32),
        pltpu.VMEM((layers, CHUNKS, 1, LANES), F32),
        pltpu.VMEM((CHUNKS,) + tile, F32),
        pltpu.VMEM((CHUNKS,) + tile, BF16),
        pltpu.VMEM(tile, BF16),
        pltpu.VMEM(tile, BF16),
        pltpu.VMEM(message, BF16),
        pltpu.VMEM(message, BF16),
        pltpu.VMEM((steps, CHUNKS, 1, LANES), F32),
        pltpu.VMEM((steps, CHUNKS, width, 1, LANES), F32),
        pltpu.VMEM((CHUNKS, 3, 1, LANES), F32),
        pltpu.VMEM((CHUNKS, width, 3, 1, LANES), F32),
        pltpu.VMEM((2, blocks, bs, bs), F32),
        pltpu.VMEM((2, layers, 2, blocks, bs, bs), BF16),
        pltpu.VMEM((layers, 2, 4, 2, bs, bs), BF16),
        pltpu.VMEM((layers, 2, 2, bs, bs), F32),
        pltpu.VMEM((tok, feat), BF16),
        pltpu.VMEM((tok, feat), BF16),
        dma((steps, CHUNKS)),
        dma((steps, CHUNKS)),
        dma((steps, CHUNKS)),
        dma((steps, CHUNKS)),
        dma((CHUNKS,)),
        dma((CHUNKS,)),
        dma,
        dma((2, layers, 2)),
        dma((3,)),
        dma((2,)),
        dma((3,)),
        dma((3,)),
        dma((2, layers, 2)),
        dma((layers, 2)),
        dma,
        dma,
        dma,
        dma,
        dma,
    ]
    grad_shape = jax.ShapeDtypeStruct((layers, blocks, bs, bs), F32)
    d_patches, grad_left, grad_right = pl.pallas_call(
        functools.partial(kernel, width, layers, blocks, total_tokens),
        out_shape=(jax.ShapeDtypeStruct((tok, feat), BF16), grad_shape, grad_shape),
        in_specs=[vmem] * 6,
        out_specs=(vmem, anyspace, anyspace),
        scratch_shapes=scratch,
        compiler_params=pltpu.CompilerParams(
            collective_id=0, has_side_effects=True, vmem_limit_bytes=60 * 1024 * 1024
        ),
        name="critics",
    )(patches, teacher, critic_pairs, left_factors[0], right_factors[0], norm_gains[0])
    return d_patches, grad_left[None], grad_right[None]


def solution(mesh):
    in_specs = (
        P(("section", "dp"), "tensor"),
        P(("section", "dp"), "tensor"),
        P(("section", "dp"), None),
        P("section", None, "tensor", None, None),
        P("section", None, "tensor", None, None),
        P("section", None, "tensor"),
    )
    out_specs = (
        P(("section", "dp"), "tensor"),
        P("section", None, "tensor", None, None),
        P("section", None, "tensor", None, None),
    )
    body = functools.partial(shards, mesh.shape["tensor"])
    return jax.shard_map(body, mesh=mesh, in_specs=in_specs, out_specs=out_specs, check_vma=False)
```

time: 731 us -> 90.8 us (0.12)
  blocking collectives: 306 us -> 0 us
  waiting for transfers between devices: 188 us -> 0 us
  Pallas kernels: 0 us -> 83.5 us
  starting transfers between devices: 77.9 us -> 0 us
  local copies, waits for them, and re-layouts: 63 us -> 6.42 us
  matrix products: 48.4 us -> 0 us
  other arithmetic: 25.9 us -> 0 us
  between operations: 15.1 us -> 0.65 us
    psum x10 -> x0, blocking collectives: 306 us -> none  [the longest x5 157 us: norm_pair(): lax.psum((jnp.sum(residuals[0] * residuals[0], axis=(1, 2)), jnp.sum(resi...]
    all_to_all x20 -> x0, waiting for transfers between devices: 99.5 us -> none  [the longest x4 24.2 us: shards(): lax.all_to_all(back_moved[0], 'tensor', split_axis=1, concat_axis=2, tile...]
    psum x1 -> x0, waiting for transfers between devices: 88.9 us -> none  [shards(): lax.psum(layer_left.astype(jnp.bfloat16), 'dp').astype(jnp.float32)]
    pallas_call x0 -> x1, Pallas kernels: none -> 83.5 us  [shards(): pl.pallas_call(functools.partial(kernel, width, layers, blocks, total_tok...]
    all_to_all x20 -> x0, starting transfers between devices: 77.9 us -> none  [the longest x4 15.8 us: shards(): lax.all_to_all(back_moved[0], 'tensor', split_axis=1, concat_axis=2, tile...]
    dot_general x48 -> x0, matrix products: 48.4 us -> none  [the longest x8 10.9 us: shards(): jnp.einsum('nkj,kij->nki', arrived[member], left_sets[member][layer_index...]
    convert_element_type x12 -> x0, other arithmetic: 15.8 us -> none  [the longest x6 14 us: shards(): (gradients[member] * gelu_slope(mixture[member])).astype(jnp.bfloat16)]
    reshape x19 -> x0, local copies, waits for them, and re-layouts: 13.7 us -> none  [the longest x8 6.85 us: shards(): back_moved = [jnp.einsum('nml,mpkl->nkmp', slopes[member], right_quads[me...]
  transfers between devices with their start and end apart: 21 -> 0, of which waited for: 20 -> 0; matrix products, arithmetic and copies ran while one was open for 7% -> 0% of each run, Pallas kernels for 0% -> 0%
where the time goes in v1:
time: 90.8 us; the launch traced here: 90.6 us
  Pallas kernels  83.5 us (92%)
  local copies, waits for them, and re-layouts  6.42 us (7%)
    pallas_call x1, Pallas kernels, shards(): pl.pallas_call(functools.partial(kernel, width, layers, blocks, total_tok...  83.5 us
    unnamed x8, local copies, waits for them, and re-layouts  6.42 us

profile of v1, /device:TPU:1, one launch (start us, length us, event | category | flops | bytes accessed | tf_op | source)
XLA Modules:
  0.0 90.6 jit_solution(12444387041207825627)
XLA Ops:
  0.6 0.0 copy-start.1
  0.6 0.7 copy-done.1
  1.3 0.8 copy.9.pairs
  2.1 83.5 %critics.1 = (bf16[192,512]{1,0:T(8,128)(2,1)}, f32[4,4,128,128]{3,2,1,0:T(8,128)}, f32[4,4,128,128]{3,2,1,0:T(8,128)}) custom-call(bf16[192,512]{1,0:T(8,128)(2,1)} %patches.1, bf16[192,512]{1,0:T(8,128)(2,1)} %teacher.1, s32[192,2]{1,0:T(8,128)} %copy.9.pairs, bf16[4,4,128,128]{3,2,1,0:T(8,128)(2,1)} %bitcast.7, bf16[4,4,128,128]{3,2,1,0:T(8,128)(2,1)} %bitcast.8, ...), custom_call_target="tpu_custom_call" | custom-call | tf_op jit(solution)/shard_map/critics/pallas_call | solution.py:619
  85.6 1.6 %copy.13 = bf16[192,512]{1,0:T(8,128)(2,1)} copy(bf16[192,512]{1,0:T(8,128)(2,1)} %get-tuple-element.12) | data formatting | bytes 393216
  87.2 0.0 copy-start
  87.2 2.4 %copy.14 = f32[1,4,4,128,128]{4,3,2,1,0:T(8,128)} copy(f32[1,4,4,128,128]{4,3,2,1,0:T(8,128)} %bitcast.6) | data formatting | bytes 2097152
  89.6 0.0 copy-done
  89.6 1.0 %copy.15 = f32[1,4,4,128,128]{4,3,2,1,0:T(8,128)} copy(f32[1,4,4,128,128]{4,3,2,1,0:T(8,128)S(1)} %bitcast.5) | data formatting | bytes 2097152
Async XLA Ops:
  0.6 0.7 copy-start.1
  87.2 2.4 %copy-start = (f32[4,4,128,128]{3,2,1,0:T(8,128)S(1)}, f32[4,4,128,128]{3,2,1,0:T(8,128)}, u32[]{:S(2)}) copy-start(f32[4,4,128,128]{3,2,1,0:T(8,128)} %get-tuple-element.8) | copy-start | bytes 3145732

commit v2 on v1

--- a/solution.py
+++ b/solution.py
@@ -49,6 +49,9 @@
     d_out,
     gl_out,
     gr_out,
+    own_p,
+    own_t,
+    own_i,
     raw_p,
     raw_t,
     raw_i,
@@ -75,7 +78,6 @@
     st_r,
     fst_s,
     fst_r,
-    gacc,
     gsend,
     grecv,
     fin,
@@ -100,6 +102,7 @@
     o_r,
     e_s,
     e_r,
+    in_s,
 ):
     x = lax.axis_index("section")
     t = lax.axis_index("tensor")
@@ -114,15 +117,28 @@
     fold = bs // all_blocks
     partner = {"dp": 1 - d}
 
+    def hops(i):
+        return sum(min(part, 4 - part) if part != 3 else 1 for part in (i >> 2, i & 3))
+
+    far_first = sorted(range(1, width), key=lambda i: -hops(i))
+
+    def peer_at(i):
+        return jnp.bitwise_xor(t, i)
+
+    loads = [
+        pltpu.make_async_copy(src, dst, in_s.at[at])
+        for at, (src, dst) in enumerate(((pairs, own_i), (patches, own_p), (teacher, own_t)))
+    ]
+    for load in loads:
+        load.start()
+
+    slot_here = x // 2
+    runs_here = lax.rem(x, 2) == d
+
     barrier = pltpu.get_barrier_semaphore()
 
-    def greet(i, _):
-        pl.semaphore_signal(
-            barrier, inc=1, device_id={"tensor": lax.rem(t + i, width)}, device_id_type=MESH
-        )
-        return 0
-
-    lax.fori_loop(1, width, greet, 0)
+    for i in far_first:
+        pl.semaphore_signal(barrier, inc=1, device_id={"tensor": peer_at(i)}, device_id_type=MESH)
     pl.semaphore_signal(barrier, inc=1, device_id=partner, device_id_type=MESH)
     for dx in range(1, sections):
         for e in range(2):
@@ -133,6 +149,19 @@
                 device_id_type=MESH,
             )
 
+    @pl.when(runs_here)
+    def _():
+        pltpu.make_async_copy(gains_in, graw.at[slot_here], n_r.at[slot_here]).start()
+
+        def take(layer, _):
+            for f, src in enumerate((left, right)):
+                pltpu.make_async_copy(
+                    src.at[layer], wbuf.at[slot_here, layer, f], w_r.at[slot_here, layer, f]
+                ).start()
+            return 0
+
+        lax.fori_loop(0, layers, take, 0)
+
     def column_of(r):
         m = r >> 7
         w = r & (bs - 1)
@@ -150,47 +179,48 @@
 
     lax.fori_loop(0, blocks, fill_perm, 0)
     gpad[...] = jnp.zeros_like(gpad)
-    gacc[...] = jnp.zeros_like(gacc)
-
-    lower = jnp.where(
-        lax.broadcasted_iota(jnp.int32, (tok, tok), 0)
-        > lax.broadcasted_iota(jnp.int32, (tok, tok), 1),
-        1.0,
-        0.0,
-    ).astype(BF16)
-    lane = lax.broadcasted_iota(jnp.int32, (tok, LANES), 1)
+
+    row_at = lax.broadcasted_iota(jnp.int32, (tok, tok), 0)
+    col_at = lax.broadcasted_iota(jnp.int32, (tok, tok), 1)
+    lower = jnp.where(row_at > col_at, 1.0, 0.0).astype(BF16)
+    same = jnp.where(row_at == col_at, 1.0, 0.0).astype(BF16)
+    lane = lax.broadcasted_iota(jnp.int32, (tok, LANES), 1).astype(F32)
 
     def one_hot(ids, critic, offset):
-        named = jnp.where((ids[:, 0:1] == critic) | (ids[:, 1:2] == critic), 1.0, 0.0)
-        named = jnp.broadcast_to(named, (tok, LANES))
-        rank = dot(lower, named.astype(BF16), NN)
-        at = lane.astype(F32) - offset
-        return jnp.where((rank == at) & (named > 0.5), 1.0, 0.0).astype(BF16)
-
-    own_ids = pairs[...]
+        named = jnp.where((ids[0:1, :] == critic) | (ids[1:2, :] == critic), 1.0, 0.0)
+        named = jnp.broadcast_to(named, (LANES, tok)).astype(BF16)
+        rank = dot(lower, named, NT)
+        here = dot(same, named, NT)
+        return jnp.where((rank == lane - offset) & (here > 0.5), 1.0, 0.0).astype(BF16)
+
+    loads[0].wait()
+    own_ids = own_i[...]
     hot[0] = one_hot(own_ids, d, 0.0)
     hot[2] = one_hot(own_ids, d + 2, 0.0)
-    hbuf[0, 0] = dot(patches[...], hot[0], TN)
-    tbuf[0] = dot(teacher[...], hot[0], TN).astype(BF16)
+    loads[1].wait()
+    hbuf[0, 0] = dot(own_p[...], hot[0], TN)
+    hbuf[0, 2] = dot(own_p[...], hot[2], TN)
 
     pl.semaphore_wait(barrier, (width - 1) + 1 + 2 * (sections - 1))
 
     raws = ((pairs, raw_i), (patches, raw_p), (teacher, raw_t))
-    for at, (src, dst) in enumerate(raws):
+
+    def send_raw(at):
         pltpu.make_async_remote_copy(
-            src_ref=src,
-            dst_ref=dst,
+            src_ref=raws[at][0],
+            dst_ref=raws[at][1],
             send_sem=raw_s.at[at],
             recv_sem=raw_r.at[at],
             device_id=partner,
             device_id_type=MESH,
         ).start()
 
-    slot_here = x // 2
-    runs_here = lax.rem(x, 2) == d
+    send_raw(0)
+    send_raw(1)
+
     half = pl.ds(2 * d, 2)
     lane_half = pl.ds(pl.multiple_of(d * (feat // 2), LANES), feat // 2)
-    for dx in range(1, sections):
+    for dx in (2, 1, 3):
         pltpu.make_async_remote_copy(
             src_ref=gains_in.at[:, lane_half],
             dst_ref=graw.at[slot_here, :, lane_half],
@@ -214,37 +244,21 @@
         return 0
 
     lax.fori_loop(0, layers, send_factors, 0)
-
-    @pl.when(runs_here)
-    def _():
-        pltpu.make_async_copy(gains_in, graw.at[slot_here], n_r.at[slot_here]).start()
-
-        def take(layer, _):
-            for f, src in enumerate((left, right)):
-                pltpu.make_async_copy(
-                    src.at[layer], wbuf.at[slot_here, layer, f], w_r.at[slot_here, layer, f]
-                ).start()
-            return 0
-
-        lax.fori_loop(0, layers, take, 0)
+    send_raw(2)
 
     def await_bytes(ref, sem):
         pltpu.make_async_copy(ref, ref, sem).wait()
 
-    def spread_gains(j):
+    def spread_gains(j, layer):
+        pick = jnp.where(
+            lax.broadcasted_iota(jnp.int32, (16, LANES), 0) == layer, 1.0, 0.0
+        ).astype(BF16)
+        gains[j, layer] = dot(gpad[j], pick, TN)
+
+    def first_gain(j):
         await_bytes(graw.at[j], n_r.at[j])
         gpad[j, 0 : layers + 1, :] = graw[j]
-
-        def one(layer, _):
-            pick = jnp.where(
-                lax.broadcasted_iota(jnp.int32, (16, LANES), 0) == layer, 1.0, 0.0
-            ).astype(BF16)
-            gains[j, layer] = dot(gpad[j], pick, TN)
-            return 0
-
-        lax.fori_loop(0, layers + 1, one, 0)
-
-    spread_gains(0)
+        spread_gains(j, 0)
 
     await_bytes(raw_i, raw_r.at[0])
     other_ids = raw_i[...]
@@ -252,12 +266,13 @@
     hot[3] = one_hot(other_ids, d + 2, float(LANES // 2))
     await_bytes(raw_p, raw_r.at[1])
     hbuf[0, 1] = dot(raw_p[...], hot[1], TN)
-    hbuf[0, 2] = dot(patches[...], hot[2], TN) + dot(raw_p[...], hot[3], TN)
-    spread_gains(1)
+    hbuf[0, 2] = hbuf[0, 2] + dot(raw_p[...], hot[3], TN)
+    first_gain(0)
+    first_gain(1)
 
     def exchange(step, q):
-        def one(i, _):
-            peer = lax.rem(t + i, width)
+        for i in far_first:
+            peer = peer_at(i)
             pltpu.make_async_remote_copy(
                 src_ref=st_s.at[step, q],
                 dst_ref=st_r.at[step, q, t],
@@ -274,9 +289,6 @@
                 device_id={"tensor": peer},
                 device_id_type=MESH,
             ).start()
-            return 0
-
-        lax.fori_loop(1, width, one, 0)
         pltpu.make_async_copy(st_s.at[step, q], st_r.at[step, q, t], t_r.at[step, q]).start()
         pltpu.make_async_copy(amsg.at[step, q, t], zrecv.at[step, q, t], m_r.at[step, q]).start()
 
@@ -325,9 +337,17 @@
 
     lax.fori_loop(0, CHUNKS, first, 0)
 
+    def more_gains(layer, _):
+        spread_gains(0, layer)
+        spread_gains(1, layer)
+        return 0
+
+    lax.fori_loop(1, layers + 1, more_gains, 0)
+    loads[2].wait()
     await_bytes(raw_t, raw_r.at[2])
+    tbuf[0] = dot(own_t[...], hot[0], TN).astype(BF16)
     tbuf[1] = dot(raw_t[...], hot[1], TN).astype(BF16)
-    tbuf[2] = (dot(teacher[...], hot[2], TN) + dot(raw_t[...], hot[3], TN)).astype(BF16)
+    tbuf[2] = (dot(own_t[...], hot[2], TN) + dot(raw_t[...], hot[3], TN)).astype(BF16)
 
     def forward(i, _):
         layer = i // CHUNKS
@@ -347,18 +367,15 @@
         fst_s[q, 1] = jnp.sum(gh * gh, axis=0, keepdims=True)
         fst_s[q, 2] = jnp.sum(gh * tbuf[q].astype(F32), axis=0, keepdims=True)
 
-        def one(i, _):
+        for i in far_first:
             pltpu.make_async_remote_copy(
                 src_ref=fst_s.at[q],
                 dst_ref=fst_r.at[q, t],
                 send_sem=f_s.at[q],
                 recv_sem=f_r.at[q],
-                device_id={"tensor": lax.rem(t + i, width)},
+                device_id={"tensor": peer_at(i)},
                 device_id_type=MESH,
             ).start()
-            return 0
-
-        lax.fori_loop(1, width, one, 0)
         pltpu.make_async_copy(fst_s.at[q], fst_r.at[q, t], f_r.at[q]).start()
         return 0
 
@@ -387,27 +404,31 @@
                 ).start()
 
     def factor_grad(layer, f, q, lhs, rhs):
-        j = q // 2
-        for k in range(blocks):
-            part = slice(k * bs, (k + 1) * bs)
-            term = dot(lhs[layer, q, part, :], rhs[part, :], NT)
-            term = term + jnp.where(q == 1, gacc[f, k], 0.0)
-            gacc[f, k] = term
-            gsend[j, layer, f, k] = term.astype(BF16)
-
-        @pl.when(q != 0)
+        @pl.when(q == 1)
         def _():
-            send_grad(layer, f, j)
+            for k in range(blocks):
+                part = slice(k * bs, (k + 1) * bs)
+                acts = jnp.concatenate((lhs[layer, 0, part, :], lhs[layer, 1, part, :]), axis=1)
+                backs = jnp.concatenate((rhs[0, part, :], rhs[1, part, :]), axis=1)
+                gsend[0, layer, f, k] = dot(acts, backs, NT).astype(BF16)
+            send_grad(layer, f, 0)
+
+        @pl.when(q == 2)
+        def _():
+            for k in range(blocks):
+                part = slice(k * bs, (k + 1) * bs)
+                gsend[1, layer, f, k] = dot(lhs[layer, 2, part, :], rhs[2, part, :], NT).astype(BF16)
+            send_grad(layer, f, 1)
 
     def bwd_send(layer, q):
         j = q // 2
         step = layers + layer
         gbs = gbuf[q] * slope[layer, q] * sbuf[layer, q]
         st_s[step, q] = jnp.sum(gbs * bbuf[layer, q], axis=0, keepdims=True)
-        gb16[...] = gbs.astype(BF16)
+        gb16[q] = gbs.astype(BF16)
         outs = []
         for m in range(blocks):
-            out = dot(wbuf[j, layer, 1, m], gb16[m * bs : (m + 1) * bs, :], NN)
+            out = dot(wbuf[j, layer, 1, m], gb16[q, m * bs : (m + 1) * bs, :], NN)
             outs.append(out.astype(BF16))
         moved = dot(perm_t[...], jnp.concatenate(outs, axis=0), NN)
         amsg[step, q] = moved.astype(BF16).reshape(width, blocks * rows, LANES)
@@ -423,8 +444,8 @@
         arrived = zrecv[step, q].astype(F32).reshape(width, blocks, rows, LANES)
         for k in range(blocks):
             part = slice(k * bs, (k + 1) * bs)
-            ga16[part, :] = arrived[:, k].reshape(bs, LANES).astype(BF16)
-            gu = dot(wbuf[j, layer, 0, k], ga16[part, :], NN)
+            ga16[q, part, :] = arrived[:, k].reshape(bs, LANES).astype(BF16)
+            gu = dot(wbuf[j, layer, 0, k], ga16[q, part, :], NN)
             gbuf[q, part, :] = (
                 gbuf[q, part, :]
                 + gu * gains[j, layer, part, :]
@@ -475,9 +496,9 @@
         factor_grad(layer, 0, q, hg, ga16)
         factor_grad(layer - 1, 1, q, zn, gb16)
 
-        @pl.when((q == CHUNKS - 1) & (layer < layers - 1))
+        @pl.when((q == CHUNKS - 1) & (layer == 1))
         def _():
-            finish(layer + 1)
+            finish(3)
 
         return 0
 
@@ -486,6 +507,11 @@
     def ending(q, _):
         bwd_take(0, q)
         factor_grad(0, 0, q, hg, ga16)
+
+        @pl.when(q == 1)
+        def _():
+            finish(2)
+
         return 0
 
     lax.fori_loop(0, CHUNKS, ending, 0)
@@ -525,7 +551,7 @@
 
     lax.fori_loop(0, CHUNKS, drain_final, 0)
     for at, (src, dst) in enumerate(raws):
-        await_bytes(src, raw_s.at[at])
+        await_bytes(dst, raw_s.at[at])
     await_bytes(wbuf.at[:, pl.ds(0, 3)], w_s)
     for at in range(sections - 1):
         await_bytes(graw.at[0, :, pl.ds(0, feat // 2)], n_s.at[at])
@@ -549,6 +575,47 @@
     await_bytes(fin, o_l)
     await_bytes(fin, o_s)
     await_bytes(fin, o_r)
+
+
+def publish_kernel(d_in, gl_in, gr_in, d_out, gl_out, gr_out, d_v, g_v, in_s, out_s):
+    layers = gl_in.shape[0]
+    moves = [(d_in, d_v, d_out)]
+    for f, (src, dst) in enumerate(((gl_in, gl_out), (gr_in, gr_out))):
+        for layer in range(layers):
+            moves.append((src.at[layer], g_v.at[f, layer], dst.at[layer]))
+    takes = [
+        pltpu.make_async_copy(src, mid, in_s.at[at]) for at, (src, mid, _) in enumerate(moves)
+    ]
+    gives = [
+        pltpu.make_async_copy(mid, dst, out_s.at[at]) for at, (_, mid, dst) in enumerate(moves)
+    ]
+    for take in takes:
+        take.start()
+    for take, give in zip(takes, gives):
+        take.wait()
+        give.start()
+    for give in gives:
+        give.wait()
+
+
+def publish(d_patches, grad_left, grad_right):
+    anyspace = pl.BlockSpec(memory_space=pl.ANY)
+    arrays = (d_patches, grad_left, grad_right)
+    count = 1 + 2 * grad_left.shape[0]
+    return pl.pallas_call(
+        publish_kernel,
+        out_shape=tuple(jax.ShapeDtypeStruct(a.shape, a.dtype) for a in arrays),
+        in_specs=[anyspace] * 3,
+        out_specs=(anyspace,) * 3,
+        scratch_shapes=[
+            pltpu.VMEM(d_patches.shape, d_patches.dtype),
+            pltpu.VMEM((2,) + grad_left.shape, grad_left.dtype),
+            pltpu.SemaphoreType.DMA((count,)),
+            pltpu.SemaphoreType.DMA((count,)),
+        ],
+        compiler_params=pltpu.CompilerParams(vmem_limit_bytes=60 * 1024 * 1024),
+        name="publish",
+    )(*arrays)
 
 
 def shards(width, patches, teacher, critic_pairs, left_factors, right_factors, norm_gains):
@@ -565,7 +632,10 @@
     scratch = [
         pltpu.VMEM((tok, feat), BF16),
         pltpu.VMEM((tok, feat), BF16),
-        pltpu.VMEM((tok, 2), jnp.int32),
+        pltpu.VMEM((2, tok), jnp.int32),
+        pltpu.VMEM((tok, feat), BF16),
+        pltpu.VMEM((tok, feat), BF16),
+        pltpu.VMEM((2, tok), jnp.int32),
         pltpu.VMEM((2, layers, 2, blocks, bs, bs), BF16),
         pltpu.VMEM((2, layers + 1, feat), BF16),
         pltpu.VMEM((2, 16, feat), BF16),
@@ -581,15 +651,14 @@
         pltpu.VMEM((layers, CHUNKS, 1, LANES), F32),
         pltpu.VMEM((CHUNKS,) + tile, F32),
         pltpu.VMEM((CHUNKS,) + tile, BF16),
-        pltpu.VMEM(tile, BF16),
-        pltpu.VMEM(tile, BF16),
+        pltpu.VMEM((CHUNKS,) + tile, BF16),
+        pltpu.VMEM((CHUNKS,) + tile, BF16),
         pltpu.VMEM(message, BF16),
         pltpu.VMEM(message, BF16),
         pltpu.VMEM((steps, CHUNKS, 1, LANES), F32),
         pltpu.VMEM((steps, CHUNKS, width, 1, LANES), F32),
         pltpu.VMEM((CHUNKS, 3, 1, LANES), F32),
         pltpu.VMEM((CHUNKS, width, 3, 1, LANES), F32),
-        pltpu.VMEM((2, blocks, bs, bs), F32),
         pltpu.VMEM((2, layers, 2, blocks, bs, bs), BF16),
         pltpu.VMEM((layers, 2, 4, 2, bs, bs), BF16),
         pltpu.VMEM((layers, 2, 2, bs, bs), F32),
@@ -614,19 +683,21 @@
         dma,
         dma,
         dma,
+        dma((3,)),
     ]
     grad_shape = jax.ShapeDtypeStruct((layers, blocks, bs, bs), F32)
     d_patches, grad_left, grad_right = pl.pallas_call(
         functools.partial(kernel, width, layers, blocks, total_tokens),
         out_shape=(jax.ShapeDtypeStruct((tok, feat), BF16), grad_shape, grad_shape),
-        in_specs=[vmem] * 6,
+        in_specs=[anyspace] * 6,
         out_specs=(vmem, anyspace, anyspace),
         scratch_shapes=scratch,
         compiler_params=pltpu.CompilerParams(
             collective_id=0, has_side_effects=True, vmem_limit_bytes=60 * 1024 * 1024
         ),
         name="critics",
-    )(patches, teacher, critic_pairs, left_factors[0], right_factors[0], norm_gains[0])
+    )(patches, teacher, critic_pairs.T, left_factors[0], right_factors[0], norm_gains[0])
+    d_patches, grad_left, grad_right = publish(d_patches, grad_left, grad_right)
     return d_patches, grad_left[None], grad_right[None]
 
 

time: 90.8 us -> 80.8 us (0.89)
  local copies, waits for them, and re-layouts: 6.42 us -> 0 us
  Pallas kernels: 83.5 us -> 80 us
    unnamed x8 -> x0, local copies, waits for them, and re-layouts: 6.42 us -> none
    pallas_call x1, Pallas kernels: 83.5 us -> 77.5 us  [shards(): pl.pallas_call(functools.partial(kernel, width, layers, blocks, total_tok...]
    pallas_call x0 -> x1, Pallas kernels: none -> 2.52 us  [publish(): pl.pallas_call(publish_kernel, out_shape=tuple((jax.ShapeDtypeStruct(a.sh...]
where the time goes in v2:
time: 80.8 us; the launch traced here: 80.6 us
  Pallas kernels  80 us (99%)
    pallas_call x1, Pallas kernels, shards(): pl.pallas_call(functools.partial(kernel, width, layers, blocks, total_tok...  77.5 us
    pallas_call x1, Pallas kernels, publish(): pl.pallas_call(publish_kernel, out_shape=tuple((jax.ShapeDtypeStruct(a.sh...  2.52 us

profile of v2, /device:TPU:1, one launch (start us, length us, event | category | flops | bytes accessed | tf_op | source)
XLA Modules:
  0.0 80.6 jit_solution(6033058793695730622)
XLA Ops:
  0.6 77.5 %critics.1 = (bf16[192,512]{1,0:T(8,128)(2,1)}, f32[4,4,128,128]{3,2,1,0:T(8,128)}, f32[4,4,128,128]{3,2,1,0:T(8,128)}) custom-call(bf16[192,512]{1,0:T(8,128)(2,1)} %patches.1, bf16[192,512]{1,0:T(8,128)(2,1)} %teacher.1, s32[2,192]{1,0:T(2,128)} %bitcast.9, bf16[4,4,128,128]{3,2,1,0:T(8,128)(2,1)} %bitcast.6, bf16[4,4,128,128]{3,2,1,0:T(8,128)(2,1)} %bitcast.7, ...), custom_call_target="tpu_custom_call" | custom-call | tf_op jit(solution)/shard_map/critics/pallas_call | solution.py:689
  78.1 2.5 %publish.1 = (bf16[192,512]{1,0:T(8,128)(2,1)}, f32[4,4,128,128]{3,2,1,0:T(8,128)}, f32[4,4,128,128]{3,2,1,0:T(8,128)}) custom-call(bf16[192,512]{1,0:T(8,128)(2,1)} %get-tuple-element.9.d_in, f32[4,4,128,128]{3,2,1,0:T(8,128)} %get-tuple-element.10.gl_in, f32[4,4,128,128]{3,2,1,0:T(8,128)} %get-tuple-element.11.gr_in), custom_call_target="tpu_custom_call" | custom-call | tf_op jit(solution)/shard_map/publish/pallas_call | solution.py:605

commit v3 on v2

--- a/solution.py
+++ b/solution.py
@@ -61,6 +61,8 @@
     gains,
     perm,
     perm_t,
+    rp,
+    rpt,
     hot,
     hbuf,
     hg,
@@ -310,26 +312,37 @@
         amsg[layer, q] = message.astype(BF16)
         exchange(layer, q)
 
+    def fold_forward(layer):
+        for j in range(2):
+            await_bytes(wbuf.at[j, layer, 1], w_r.at[j, layer, 1])
+            for m in range(blocks):
+                part = slice(m * bs, (m + 1) * bs)
+                rp[j, layer, part, :] = dot(wbuf[j, layer, 1, m], perm[part, :], TN).astype(BF16)
+
+    def fold_backward(layer):
+        for j in range(2):
+            for m in range(blocks):
+                part = slice(m * bs, (m + 1) * bs)
+                rpt[j, layer, :, part] = dot(perm_t[:, part], wbuf[j, layer, 1, m], NN).astype(BF16)
+
     def fwd_take(layer, q):
         j = q // 2
-
-        @pl.when(q != 1)
-        def _():
-            await_bytes(wbuf.at[j, layer, 1], w_r.at[j, layer, 1])
-
         await_bytes(st_r.at[layer, q], t_r.at[layer, q])
         await_bytes(zrecv.at[layer, q], m_r.at[layer, q])
         squares = jnp.sum(st_r[layer, q], axis=0)
         s = lax.rsqrt(squares / model + EPSILON)
         sbuf[layer, q] = s
-        zn[layer, q] = dot(perm[...], zrecv[layer, q].reshape(feat, LANES), NN).astype(BF16)
+        arrived = zrecv[layer, q].reshape(feat, LANES)
         for m in range(blocks):
             part = slice(m * bs, (m + 1) * bs)
-            b = dot(wbuf[j, layer, 1, m], zn[layer, q, part, :], TN) * s
+            b = dot(rp[j, layer, part, :], arrived, NN) * s
             bbuf[layer, q, part, :] = b
             value, steep = gelu_both(b)
             slope[layer, q, part, :] = steep
             hbuf[layer + 1, q, part, :] = hbuf[layer, q, part, :] + value
+
+    def keep_z(layer, q):
+        zn[layer, q] = dot(perm[...], zrecv[layer, q].reshape(feat, LANES), NN).astype(BF16)
 
     def first(q, _):
         fwd_send(0, q)
@@ -349,11 +362,19 @@
     tbuf[1] = dot(raw_t[...], hot[1], TN).astype(BF16)
     tbuf[2] = (dot(own_t[...], hot[2], TN) + dot(raw_t[...], hot[3], TN)).astype(BF16)
 
+    fold_forward(0)
+
     def forward(i, _):
         layer = i // CHUNKS
         q = lax.rem(i, CHUNKS)
         fwd_take(layer, q)
         fwd_send(layer + 1, q)
+        keep_z(layer, q)
+
+        @pl.when(q == CHUNKS - 1)
+        def _():
+            fold_forward(layer + 1)
+
         return 0
 
     lax.fori_loop(0, CHUNKS * (layers - 1), forward, 0)
@@ -377,9 +398,12 @@
                 device_id_type=MESH,
             ).start()
         pltpu.make_async_copy(fst_s.at[q], fst_r.at[q, t], f_r.at[q]).start()
+        keep_z(layers - 1, q)
         return 0
 
     lax.fori_loop(0, CHUNKS, last, 0)
+    fold_backward(layers - 1)
+    fold_backward(layers - 2)
 
     def send_grad(layer, f, j):
         critic = d + 2 * j
@@ -426,25 +450,25 @@
         gbs = gbuf[q] * slope[layer, q] * sbuf[layer, q]
         st_s[step, q] = jnp.sum(gbs * bbuf[layer, q], axis=0, keepdims=True)
         gb16[q] = gbs.astype(BF16)
-        outs = []
-        for m in range(blocks):
-            out = dot(wbuf[j, layer, 1, m], gb16[q, m * bs : (m + 1) * bs, :], NN)
-            outs.append(out.astype(BF16))
-        moved = dot(perm_t[...], jnp.concatenate(outs, axis=0), NN)
+        moved = dot(rpt[j, layer], gb16[q], NN)
         amsg[step, q] = moved.astype(BF16).reshape(width, blocks * rows, LANES)
         exchange(step, q)
 
-    def bwd_take(layer, q):
-        j = q // 2
+    def bwd_land(layer, q):
         step = layers + layer
         await_bytes(st_r.at[step, q], t_r.at[step, q])
         await_bytes(zrecv.at[step, q], m_r.at[step, q])
-        inner = jnp.sum(st_r[step, q], axis=0)
-        coefficient = sbuf[layer, q] * inner / model
         arrived = zrecv[step, q].astype(F32).reshape(width, blocks, rows, LANES)
         for k in range(blocks):
             part = slice(k * bs, (k + 1) * bs)
             ga16[q, part, :] = arrived[:, k].reshape(bs, LANES).astype(BF16)
+
+    def bwd_norm(layer, q):
+        j = q // 2
+        inner = jnp.sum(st_r[layers + layer, q], axis=0)
+        coefficient = sbuf[layer, q] * inner / model
+        for k in range(blocks):
+            part = slice(k * bs, (k + 1) * bs)
             gu = dot(wbuf[j, layer, 0, k], ga16[q, part, :], NN)
             gbuf[q, part, :] = (
                 gbuf[q, part, :]
@@ -456,7 +480,7 @@
     outs = (gl_out, gr_out)
 
     def finish(layer):
-        for f in range(2):
+        for f in (1, 0):
             await_bytes(grecv.at[layer, f], g_r.at[layer, f])
             total = grecv[layer, f, 0].astype(F32)
             for source in range(1, sections):
@@ -491,7 +515,8 @@
     def backward(i, _):
         layer = layers - 1 - i // CHUNKS
         q = lax.rem(i, CHUNKS)
-        bwd_take(layer, q)
+        bwd_land(layer, q)
+        bwd_norm(layer, q)
         bwd_send(layer - 1, q)
         factor_grad(layer, 0, q, hg, ga16)
         factor_grad(layer - 1, 1, q, zn, gb16)
@@ -500,13 +525,18 @@
         def _():
             finish(3)
 
+        @pl.when((q == CHUNKS - 1) & (layer > 1))
+        def _():
+            fold_backward(layer - 2)
+
         return 0
 
     lax.fori_loop(0, CHUNKS * (layers - 1), backward, 0)
 
     def ending(q, _):
-        bwd_take(0, q)
+        bwd_land(0, q)
         factor_grad(0, 0, q, hg, ga16)
+        bwd_norm(0, q)
 
         @pl.when(q == 1)
         def _():
@@ -531,9 +561,6 @@
     back.start()
     own = dot(hot[0], lead_own, NT) + dot(hot[2], trail, NT)
     finish(1)
-    back.wait()
-    d_out[...] = ((own + d_r[...].astype(F32)) * 0.5).astype(BF16)
-    finish(0)
 
     def drain(step, _):
         def one(q, _):
@@ -556,6 +583,10 @@
     for at in range(sections - 1):
         await_bytes(graw.at[0, :, pl.ds(0, feat // 2)], n_s.at[at])
 
+    back.wait()
+    d_out[...] = ((own + d_r[...].astype(F32)) * 0.5).astype(BF16)
+    finish(0)
+
     def drain_grad(layer, _):
         for j in range(2):
             for f in range(2):
@@ -577,43 +608,30 @@
     await_bytes(fin, o_r)
 
 
-def publish_kernel(d_in, gl_in, gr_in, d_out, gl_out, gr_out, d_v, g_v, in_s, out_s):
+def publish_kernel(d_in, gl_in, gr_in, d_out, gl_out, gr_out, sems):
     layers = gl_in.shape[0]
-    moves = [(d_in, d_v, d_out)]
-    for f, (src, dst) in enumerate(((gl_in, gl_out), (gr_in, gr_out))):
+    moves = [(d_in, d_out)]
+    for src, dst in ((gl_in, gl_out), (gr_in, gr_out)):
         for layer in range(layers):
-            moves.append((src.at[layer], g_v.at[f, layer], dst.at[layer]))
-    takes = [
-        pltpu.make_async_copy(src, mid, in_s.at[at]) for at, (src, mid, _) in enumerate(moves)
+            moves.append((src.at[layer], dst.at[layer]))
+    copies = [
+        pltpu.make_async_copy(src, dst, sems.at[at]) for at, (src, dst) in enumerate(moves)
     ]
-    gives = [
-        pltpu.make_async_copy(mid, dst, out_s.at[at]) for at, (_, mid, dst) in enumerate(moves)
-    ]
-    for take in takes:
-        take.start()
-    for take, give in zip(takes, gives):
-        take.wait()
-        give.start()
-    for give in gives:
-        give.wait()
-
-
-def publish(d_patches, grad_left, grad_right):
+    for copy in copies:
+        copy.start()
+    for copy in copies:
+        copy.wait()
+
+
+def publish(*arrays):
     anyspace = pl.BlockSpec(memory_space=pl.ANY)
-    arrays = (d_patches, grad_left, grad_right)
-    count = 1 + 2 * grad_left.shape[0]
     return pl.pallas_call(
         publish_kernel,
         out_shape=tuple(jax.ShapeDtypeStruct(a.shape, a.dtype) for a in arrays),
         in_specs=[anyspace] * 3,
-        out_specs=(anyspace,) * 3,
-        scratch_shapes=[
-            pltpu.VMEM(d_patches.shape, d_patches.dtype),
-            pltpu.VMEM((2,) + grad_left.shape, grad_left.dtype),
-            pltpu.SemaphoreType.DMA((count,)),
-            pltpu.SemaphoreType.DMA((count,)),
-        ],
-        compiler_params=pltpu.CompilerParams(vmem_limit_bytes=60 * 1024 * 1024),
+        out_specs=(pl.BlockSpec(memory_space=pltpu.HBM),) * 3,
+        scratch_shapes=[pltpu.SemaphoreType.DMA((1 + 2 * arrays[1].shape[0],))],
+        compiler_params=pltpu.CompilerParams(vmem_limit_bytes=16 * 1024 * 1024),
         name="publish",
     )(*arrays)
 
@@ -642,6 +660,8 @@
         pltpu.VMEM((2, layers + 1) + tile, F32),
         pltpu.VMEM((feat, feat), BF16),
         pltpu.VMEM((feat, feat), BF16),
+        pltpu.VMEM((2, layers, feat, feat), BF16),
+        pltpu.VMEM((2, layers, feat, feat), BF16),
         pltpu.VMEM((4, tok, LANES), BF16),
         pltpu.VMEM((layers + 1, CHUNKS) + tile, F32),
         pltpu.VMEM((layers, CHUNKS) + tile, BF16),
@@ -685,6 +705,14 @@
         dma,
         dma((3,)),
     ]
+    operands = (
+        patches,
+        teacher,
+        critic_pairs.T,
+        left_factors[0],
+        right_factors[0],
+        norm_gains[0],
+    )
     grad_shape = jax.ShapeDtypeStruct((layers, blocks, bs, bs), F32)
     d_patches, grad_left, grad_right = pl.pallas_call(
         functools.partial(kernel, width, layers, blocks, total_tokens),
@@ -693,10 +721,10 @@
         out_specs=(vmem, anyspace, anyspace),
         scratch_shapes=scratch,
         compiler_params=pltpu.CompilerParams(
-            collective_id=0, has_side_effects=True, vmem_limit_bytes=60 * 1024 * 1024
+            collective_id=0, has_side_effects=True, vmem_limit_bytes=48 * 1024 * 1024
         ),
         name="critics",
-    )(patches, teacher, critic_pairs.T, left_factors[0], right_factors[0], norm_gains[0])
+    )(*(pltpu.with_memory_space_constraint(a, pltpu.HBM) for a in operands))
     d_patches, grad_left, grad_right = publish(d_patches, grad_left, grad_right)
     return d_patches, grad_left[None], grad_right[None]
 

time: 80.8 us -> 77.4 us (0.958)
  Pallas kernels: 80 us -> 76.7 us
    pallas_call x1, Pallas kernels: 77.5 us -> 75.2 us  [shards(): pl.pallas_call(functools.partial(kernel, width, layers, blocks, total_tok...]
    pallas_call x1, Pallas kernels: 2.52 us -> 1.45 us  [publish(): pl.pallas_call(publish_kernel, out_shape=tuple((jax.ShapeDtypeStruct(a.sh...]
where the time goes in v3:
time: 77.4 us; the launch traced here: 77.3 us
  Pallas kernels  76.7 us (99%)
    pallas_call x1, Pallas kernels, shards(): pl.pallas_call(functools.partial(kernel, width, layers, blocks, total_tok...  75.2 us

profile of v3, /device:TPU:1, one launch (start us, length us, event | category | flops | bytes accessed | tf_op | source)
XLA Modules:
  0.0 77.3 jit_solution(2266814260946588649)
XLA Ops:
  0.6 75.2 %critics.1 = (bf16[192,512]{1,0:T(8,128)(2,1)S(1)}, f32[4,4,128,128]{3,2,1,0:T(8,128)S(1)}, f32[4,4,128,128]{3,2,1,0:T(8,128)S(1)}) custom-call(bf16[192,512]{1,0:T(8,128)(2,1)} %patches.1, bf16[192,512]{1,0:T(8,128)(2,1)} %teacher.1, s32[2,192]{1,0:T(2,128)} %bitcast.9, bf16[4,4,128,128]{3,2,1,0:T(8,128)(2,1)} %bitcast.6, bf16[4,4,128,128]{3,2,1,0:T(8,128)(2,1)} %bitcast.7, ...), custom_call_target="tpu_custom_call" | custom-call | tf_op jit(solution)/shard_map/critics/pallas_call | solution.py:717
  75.9 1.5 %publish.1 = (bf16[192,512]{1,0:T(8,128)(2,1)}, f32[4,4,128,128]{3,2,1,0:T(8,128)}, f32[4,4,128,128]{3,2,1,0:T(8,128)}) custom-call(bf16[192,512]{1,0:T(8,128)(2,1)S(1)} %get-tuple-element.9.d_in, f32[4,4,128,128]{3,2,1,0:T(8,128)S(1)} %get-tuple-element.10.gl_in, f32[4,4,128,128]{3,2,1,0:T(8,128)S(1)} %get-tuple-element.11.gr_in), custom_call_target="tpu_custom_call" | custom-call | tf_op jit(solution)/shard_map/publish/pallas_call | solution.py:628
